TPU v7x, 128 devices: a whole 4x4x4 slice. The times are simulated.
128 devices in a mesh: owner: 4 (over y), worker: 32 (over x, z, core).
Axes of the slice: x: 4, y: 4, z: 4, core: 2. Of those that a mesh axis runs over, the one named last changes fastest.
Arguments:
- states: float32 [262144, 512], P(('owner', 'worker')), may hold values from -3 to 3
- row_of_user: int32 [262144], replicated, may hold values from 0 to 262143, as said below
- event_users: int32 [65536], P(('owner', 'worker')), may hold values from 0 to 262143, as said below
- event_features: int32 [65536], P(('owner', 'worker')), may hold values from 0 to 4095
- feature_table: bfloat16 [4096, 512], replicated, may hold values from -6 to 6
- gate_in: bfloat16 [512, 1536], replicated, may hold values from -0.25 to 0.25
- gate_state: bfloat16 [512, 1536], replicated, may hold values from -0.25 to 0.25
- tower_in: bfloat16 [4096, 1024], P(('owner', 'worker')), may hold values from -0.1875 to 0.1875
- tower_out: bfloat16 [512, 4096], P(('owner', 'worker')), may hold values from -0.09375 to 0.09375
Outputs:
- new_states: float32 [262144, 512], P(('owner', 'worker'))
- scores: float32 [65536], P(('owner', 'worker'))
Inputs may be any that keep to these rules, and one draw needn't show every extreme that they name: `row_of_user`: A permutation: each user has its own state row. `event_users`: among the 512 events of one device, at most 8 have their row (row_of_user of the user) in one device's block of 2048 rows, and for every device some block receives exactly 8 of its events.
All inputs are finite; a program needn't handle non-finite values.
Results may differ from a plain program's by a relative error of at most 0.0034.
Values may be sent and summed in bfloat16 or wider, within the bound.
A program may use at most 128 MiB of HBM per device.

v0:
```python
import jax
import jax.numpy as jnp
from jax import lax
from jax.sharding import PartitionSpec as P


def gru_cell(inputs, prior, gate_in, gate_state):
    gx = jnp.dot(inputs, gate_in, preferred_element_type=jnp.float32)
    gh = jnp.dot(prior, gate_state, preferred_element_type=jnp.float32)
    width = prior.shape[-1]
    reset = jax.nn.sigmoid(gx[:, :width] + gh[:, :width])
    update = jax.nn.sigmoid(gx[:, width : 2 * width] + gh[:, width : 2 * width])
    cand = jnp.tanh(gx[:, 2 * width :] + reset * gh[:, 2 * width :])
    return (1.0 - update) * cand + update * prior.astype(jnp.float32)


def per_device(
    states,
    row_of_user,
    event_users,
    event_features,
    feature_table,
    gate_in,
    gate_state,
    tower_in,
    tower_out,
):
    shards = lax.axis_size(("owner", "worker"))
    events = event_users.shape[0]
    row_count = states.shape[0]
    width = states.shape[1]
    cap = 2 * (events // shards)
    rows = row_of_user[event_users]
    target = rows // row_count
    local = rows - target * row_count
    inputs = feature_table[event_features]
    hits = (target[:, None] == jnp.arange(shards, dtype=jnp.int32)[None, :]).astype(jnp.int32)
    rank = jnp.sum((jnp.cumsum(hits, axis=0) - hits) * hits, axis=1)
    slot = target * cap + rank
    requests = jnp.full((shards * cap,), -1, jnp.int32).at[slot].set(local).reshape(shards, cap)
    asked = lax.all_to_all(requests, ("owner", "worker"), split_axis=0, concat_axis=0, tiled=True)
    fetched = states[jnp.maximum(asked, 0)].astype(jnp.bfloat16)
    arrived, asked = (
        lax.all_to_all(fetched, ("owner", "worker"), split_axis=0, concat_axis=0, tiled=True),
        asked,
    )
    prior = arrived.reshape(shards * cap, width)[slot]
    fresh = gru_cell(inputs, prior, gate_in, gate_state)
    fresh_low = fresh.astype(jnp.bfloat16)
    delta = fresh - prior.astype(jnp.float32)
    outgoing = (
        jnp.zeros((shards * cap, width), jnp.float32)
        .at[slot]
        .set(delta)
        .reshape(shards, cap, width)
    )
    changes = lax.all_to_all(outgoing, ("owner", "worker"), split_axis=0, concat_axis=0, tiled=True)
    valid = asked.reshape(-1) >= 0
    owners_ids = jnp.where(valid, asked.reshape(-1), row_count)
    total = jax.ops.segment_sum(changes.reshape(-1, width), owners_ids, num_segments=row_count + 1)[
        :row_count
    ]
    count = jax.ops.segment_sum(valid.astype(jnp.int32), owners_ids, num_segments=row_count + 1)[
        :row_count
    ]
    new_states = states + total / jnp.maximum(count, 1).astype(jnp.float32)[:, None]
    joined = jnp.concatenate([fresh_low, inputs], axis=1)
    hidden = jax.nn.gelu(
        lax.dot_general(
            joined,
            lax.all_gather(tower_in, ("owner", "worker"), axis=0, tiled=True),
            (((1,), (1,)), ((), ())),
            preferred_element_type=jnp.float32,
        )
    ).astype(jnp.bfloat16)
    tower = lax.dot_general(
        hidden,
        lax.all_gather(tower_out, ("owner", "worker"), axis=0, tiled=True),
        (((1,), (1,)), ((), ())),
        preferred_element_type=jnp.float32,
    )
    scores = jnp.sum(tower * inputs.astype(jnp.float32), axis=1) / jnp.sqrt(jnp.float32(width))
    return (new_states, scores)


def solution(mesh):
    placed = (
        P(("owner", "worker"), None),
        P(),
        P(("owner", "worker")),
        P(("owner", "worker")),
        P(),
        P(),
        P(),
        P(("owner", "worker"), None),
        P(("owner", "worker"), None),
    )
    return jax.shard_map(
        per_device,
        mesh=mesh,
        in_specs=placed,
        out_specs=(P(("owner", "worker"), None), P(("owner", "worker"))),
        check_vma=False,
    )
```

profile of v0, /device:TPU:1, one launch (start us, length us, event | category | flops | bytes accessed | tf_op | source)
XLA Modules:
  0.0 186.0 jit_solution(2126969948334331115)
XLA Ops:
  7.2 0.0 copy-start
  7.2 0.0 all-gather.6.cloned.1.call-start
  7.2 0.7 all-gather.6.cloned.1.call-update
  7.9 0.0 all-gather.4.cloned.1.call-start
  8.0 0.7 all-gather.4.cloned.1.call-update
  8.7 0.7 compare_select_fusion.3
  9.4 6.5 %gather_fusion = s32[512]{0:T(512)S(1)} fusion(s32[262144]{0:T(1024)} %param.10, s32[1024]{0:T(1024)S(1)} %pad_clamp_fusion.2), kind=kCustom, calls=%fused_computation | custom fusion | bytes 6144 | tf_op jit(solution)/shard_map/gather | solution.py:33
  15.9 0.1 copy.15
  16.0 0.2 fusion.46
  16.3 0.2 fusion.45
  16.6 2.4 %scatter_custom_fusion = s32[1024]{0:T(1024)S(1)} fusion(s32[512]{0:T(512)S(1)} %bitcast.59, s32[512]{0:T(512)S(1)} %get-tuple-element.7, s32[]{:T(128)} %constant.17.clone.1), kind=kCustom, calls=%fused_computation.93 | custom fusion | bytes 4100 | tf_op jit(solution)/shard_map/scatter | solution.py:40
  19.0 0.1 all_to_all.12
  19.1 20.7 %all_to_all.19 = s32[128,1,8]{2,1,0:T(1,128)S(1)} all-to-all(s32[128,1,8]{2,1,0:T(1,128)S(1)} %bitcast.54), channel_id=1, replica_groups=mesh['owner'=4,'worker'=32] {'owner','worker'}, dimensions={0} | all-to-all | bytes 8192 | tf_op jit(solution)/shard_map/all_to_all | solution.py:41
  39.8 0.5 broadcast.212
  40.4 1.2 fusion.49
  41.5 0.1 reshape.170
  41.6 0.0 copy-start.4
  41.7 7.3 %gather_fusion.2 = bf16[1024,512]{1,0:T(8,128)(2,1)} fusion(f32[2048,512]{1,0:T(8,128)} %param.9, s32[1024]{0:T(1024)S(1)} %broadcast_clamp_fusion), kind=kCustom, calls=%fused_computation.2 | custom fusion | bytes 2101248 | tf_op jit(solution)/shard_map/gather | solution.py:42
  49.0 4.6 %all-to-all-start.1 = ((bf16[128,8,512]{2,1,0:T(8,128)(2,1)}), bf16[128,8,512]{2,1,0:T(8,128)(2,1)S(1)}, u32[]{:S(2)}, u32[]{:S(2)}) async-start(bf16[128,8,512]{2,1,0:T(8,128)(2,1)} %bitcast.51), calls=%async_computation.1 | async-start | bytes 2097152 | tf_op jit(solution)/shard_map/all_to_all | solution.py:44
  53.6 0.0 copy-done.4
  53.6 4.7 %gather_fusion.1 = bf16[512,512]{1,0:T(8,128)(2,1)S(1)} fusion(bf16[4096,512]{1,0:T(8,128)(2,1)} %param.13, s32[1024]{0:T(1024)S(1)} %pad_clamp_fusion.1), kind=kCustom, calls=%fused_computation.1 | custom fusion | bytes 1050624 | tf_op jit(solution)/shard_map/gather | solution.py:36
  58.3 0.0 copy-start.2
  58.4 0.0 copy-done
  58.4 2.6 %fusion.68 = f32[512,1536]{1,0:T(8,128)} fusion(bf16[512,512]{1,0:T(8,128)(2,1)S(1)} %gather_fusion.1, bf16[512,1536]{1,0:T(8,128)(2,1)S(1)} %copy-done), kind=kOutput, calls=%fused_computation.104 | convolution fusion | flops 805306368 | bytes 5242880 | tf_op jit(solution)/shard_map/dot_general | solution.py:8
  61.0 11.9 %all-to-all-done.1 = bf16[128,8,512]{2,1,0:T(8,128)(2,1)S(1)} async-done(((bf16[128,8,512]{2,1,0:T(8,128)(2,1)}), bf16[128,8,512]{2,1,0:T(8,128)(2,1)S(1)}, u32[]{:S(2)}, u32[]{:S(2)}) %all-to-all-start.1) | async-done | bytes 1048608 | tf_op jit(solution)/shard_map/all_to_all | solution.py:44
  72.9 0.0 copy-done.2
  72.9 2.0 %gather_fusion.3 = bf16[512,512]{1,0:T(8,128)(2,1)S(1)} fusion(bf16[1024,512]{1,0:T(8,128)(2,1)S(1)} %bitcast.49, s32[1024]{0:T(1024)S(1)} %pad_clamp_fusion), kind=kCustom, calls=%fused_computation.3 | custom fusion | bytes 1050624 | tf_op jit(solution)/shard_map/gather | solution.py:47
  74.9 0.0 copy-start.1
  74.9 2.6 %fusion.69 = f32[512,1536]{1,0:T(8,128)S(1)} fusion(bf16[512,512]{1,0:T(8,128)(2,1)S(1)} %gather_fusion.3, bf16[512,1536]{1,0:T(8,128)(2,1)} %param.15), kind=kOutput, calls=%fused_computation.105 | convolution fusion | flops 805306368 | bytes 5242880 | tf_op jit(solution)/shard_map/dot_general | solution.py:9
  77.5 0.0 copy-done.1
  77.5 1.9 %fusion.66 = (bf16[512,512]{1,0:T(8,128)(2,1)S(1)}, f32[512,512]{1,0:T(8,128)}) fusion(bf16[512,512]{1,0:T(8,128)(2,1)S(1)} %gather_fusion.3, f32[512,1536]{1,0:T(8,128)S(1)} %fusion.69, f32[512,1536]{1,0:T(8,128)S(1)} %copy-done.1), kind=kLoop, calls=%fused_computation.103 | loop fusion | flops 4194304 | bytes 8388608 | tf_op jit(solution)/shard_map/convert_element_type | solution.py:49
  79.4 0.0 copy-start.3
  79.4 4.4 %scatter_custom_fusion.1 = f32[1024,512]{1,0:T(8,128)} fusion(s32[512]{0:T(512)S(1)} %bitcast.61, f32[512,512]{1,0:T(8,128)} %get-tuple-element.6, bf16[512,512]{1,0:T(8,128)(2,1)S(1)} %gather_fusion.3, f32[]{:T(128)} %constant.16.clone.1), kind=kCustom, calls=%fused_computation.28 | custom fusion | flops 524288 | bytes 3670020 | tf_op jit(solution)/shard_map/scatter | solution.py:54
  83.8 5.7 %all-to-all-start.2 = ((f32[128,8,512]{2,1,0:T(8,128)}), f32[128,8,512]{2,1,0:T(8,128)}, u32[]{:S(2)}, u32[]{:S(2)}) async-start(f32[128,8,512]{2,1,0:T(8,128)} %bitcast.50), calls=%async_computation.2 | async-start | bytes 4194304 | tf_op jit(solution)/shard_map/all_to_all | solution.py:57
  89.5 0.0 copy-done.3
  89.5 0.2 copy.18
  89.7 0.1 reshape.147
  89.8 0.1 reshape.212
  89.9 6.8 %scatter_custom_fusion.3 = s32[2049]{0:T(1024)S(1)} fusion(s32[1024]{0:T(1024)S(1)} %bitcast.62, s32[1024]{0:T(1024)S(1)} %reshape.212, s32[]{:T(128)} %constant.18.clone.1), kind=kCustom, calls=%fused_computation.66 | custom fusion | flops 1024 | bytes 8200 | tf_op jit(solution)/shard_map/scatter-add | solution.py:63
  96.7 23.3 %all-to-all-done.2 = f32[128,8,512]{2,1,0:T(8,128)} async-done(((f32[128,8,512]{2,1,0:T(8,128)}), f32[128,8,512]{2,1,0:T(8,128)}, u32[]{:S(2)}, u32[]{:S(2)}) %all-to-all-start.2) | async-done | bytes 2097184 | tf_op jit(solution)/shard_map/all_to_all | solution.py:57
  120.0 9.9 %scatter_custom_fusion.2 = f32[2049,512]{1,0:T(8,128)} fusion(s32[1024]{0:T(1024)S(1)} %bitcast.63, f32[]{:T(128)} %constant.16.clone.1, f32[128,8,512]{2,1,0:T(8,128)} %all-to-all-done.2), kind=kCustom, calls=%fused_computation.20 | custom fusion | flops 524288 | bytes 6293508 | tf_op jit(solution)/shard_map/scatter-add | solution.py:60
  129.9 6.1 %fusion.8 = f32[2048,512]{1,0:T(8,128)} fusion(f32[2048,512]{1,0:T(8,128)} %param.9, f32[2049,512]{1,0:T(8,128)} %scatter_custom_fusion.2, f32[2048]{0:T(1024)S(1)} %fusion.50), kind=kLoop, calls=%fused_computation.18 | loop fusion | flops 2097152 | bytes 12591104 | tf_op jit(solution)/shard_map/add | solution.py:66
  136.0 0.0 all-gather.6.cloned.1.call-done
  136.0 6.9 %reshape.222 = bf16[512,4096]{1,0:T(8,128)(2,1)} reshape(bf16[128,4,4096]{2,1,0:T(4,128)(2,1)} %all-gather.6.cloned.1.call-done) | data formatting | bytes 8388608
  142.9 24.2 %all-gather.4.cloned.1.call-done = bf16[4096,1024]{1,0:T(8,128)(2,1)} async-done(((bf16[32,1024]{1,0:T(8,128)(2,1)}), bf16[4096,1024]{1,0:T(8,128)(2,1)}) %all-gather.4.cloned.1.call-update) | async-done | bytes 8388624 | tf_op jit(solution)/shard_map/all_gather | solution.py:71
  167.1 11.4 %fusion.17 = f32[512]{0:T(512)S(1)} fusion(bf16[512,4096]{1,0:T(8,128)(2,1)} %reshape.222, bf16[4096,1024]{1,0:T(8,128)(2,1)} %all-gather.4.cloned.1.call-done, bf16[512,512]{1,0:T(8,128)(2,1)S(1)} %copy-done.3, bf16[512,512]{1,0:T(8,128)(2,1)S(1)} %get-tuple-element.5, bf16[512,512]{0,1:T(8,128)(2,1)S(1)} %copy.18), kind=kOutput, calls=%fused_computation.26 | convolution fusion | flops 6464208384 | bytes 14157824 | tf_op jit(solution)/shard_map/dot_general | solution.py:76
  178.6 0.6 broadcast_multiply_fusion
  (16 shorter events, 0.2 us)
Async XLA Ops:
  7.2 51.2 %copy-start = (bf16[512,1536]{1,0:T(8,128)(2,1)S(1)}, bf16[512,1536]{1,0:T(8,128)(2,1)}, u32[]{:S(2)}) copy-start(bf16[512,1536]{1,0:T(8,128)(2,1)} %param.14) | copy-start | bytes 4718596
  7.2 128.8 %all-gather.6.cloned.1.call-start = ((), (), s32[]{:S(2)}) async-start(), calls=%async_computation.4 | async-start | bytes 4227072 | tf_op jit(solution)/shard_map/all_gather | solution.py:78
  7.9 159.2 %all-gather.4.cloned.1.call-start = ((), (), s32[]{:S(2)}) async-start(), calls=%async_computation.3 | async-start | bytes 8454144 | tf_op jit(solution)/shard_map/all_gather | solution.py:71
  41.6 11.9 %copy-start.4 = (s32[512]{0:T(512)S(1)}, s32[512]{0:T(512)}, u32[]{:S(2)}) copy-start(s32[512]{0:T(512)} %param.12) | copy-start | bytes 6148
  49.0 24.0 %all-to-all-start.1 = ((bf16[128,8,512]{2,1,0:T(8,128)(2,1)}), bf16[128,8,512]{2,1,0:T(8,128)(2,1)S(1)}, u32[]{:S(2)}, u32[]{:S(2)}) async-start(bf16[128,8,512]{2,1,0:T(8,128)(2,1)} %bitcast.51), calls=%async_computation.1 | async-start | bytes 2097152 | tf_op jit(solution)/shard_map/all_to_all | solution.py:44
  58.3 14.6 %copy-start.2 = (bf16[512,512]{1,0:T(8,128)(2,1)}, bf16[512,512]{1,0:T(8,128)(2,1)S(1)}, u32[]{:S(2)}) copy-start(bf16[512,512]{1,0:T(8,128)(2,1)S(1)} %gather_fusion.1) | copy-start | bytes 1572868
  74.9 2.6 %copy-start.1 = (f32[512,1536]{1,0:T(8,128)S(1)}, f32[512,1536]{1,0:T(8,128)}, u32[]{:S(2)}) copy-start(f32[512,1536]{1,0:T(8,128)} %fusion.68) | copy-start | bytes 9437188
  79.4 10.1 %copy-start.3 = (bf16[512,512]{1,0:T(8,128)(2,1)S(1)}, bf16[512,512]{1,0:T(8,128)(2,1)}, u32[]{:S(2)}) copy-start(bf16[512,512]{1,0:T(8,128)(2,1)} %copy-done.2) | copy-start | bytes 1572868
  83.8 36.2 %all-to-all-start.2 = ((f32[128,8,512]{2,1,0:T(8,128)}), f32[128,8,512]{2,1,0:T(8,128)}, u32[]{:S(2)}, u32[]{:S(2)}) async-start(f32[128,8,512]{2,1,0:T(8,128)} %bitcast.50), calls=%async_computation.2 | async-start | bytes 4194304 | tf_op jit(solution)/shard_map/all_to_all | solution.py:57
Sparse Core Ops, SparseCore 0:
  11.2 73.3 all-gather.5
  87.6 79.5 all-gather.3
where the time goes:
time: 187 us; the launch traced here: 186 us
  waiting for transfers between devices  60.9 us (33%)
  other arithmetic  32.1 us (17%)
  local copies, waits for them, and re-layouts  31.1 us (17%)
  blocking collectives  20.7 us (11%)
  matrix products  16.6 us (9%)
  between operations  14.3 us (8%)
  starting transfers between devices  10.3 us (6%)
    all_gather x1, waiting for transfers between devices, per_device(): lax.all_gather(tower_in, ('owner', 'worker'), axis=0, tiled=True)  24.2 us
    all_to_all x1, waiting for transfers between devices, per_device(): lax.all_to_all(outgoing, ('owner', 'worker'), split_axis=0, concat_axis=0...  23.3 us
    all_to_all x1, blocking collectives, per_device(): lax.all_to_all(requests, ('owner', 'worker'), split_axis=0, concat_axis=0...  20.7 us
    all_to_all x1, waiting for transfers between devices, per_device(): lax.all_to_all(fetched, ('owner', 'worker'), split_axis=0, concat_axis=0,...  11.9 us
    dot_general x1, matrix products, per_device(): lax.dot_general(hidden, lax.all_gather(tower_out, ('owner', 'worker'), ax...  11.4 us
    scatter-add x1, other arithmetic, per_device(): jax.ops.segment_sum(changes.reshape(-1, width), owners_ids, num_segments=...  9.86 us
    gather x1, local copies, waits for them, and re-layouts, per_device(): fetched = states[jnp.maximum(asked, 0)].astype(jnp.bfloat16)  7.29 us
    unnamed x12, local copies, waits for them, and re-layouts  6.96 us
  transfers between devices with their start and end apart: 4, of which 3 were waited for; matrix products, arithmetic and copies ran while one was open for 36% of the time, Pallas kernels for 0%

commit v1 on v0

v1 whole, which is shorter than its diff:
```python
import jax
import jax.numpy as jnp
from jax import lax
from jax.sharding import PartitionSpec as P

AXES = ("owner", "worker")


def gru_cell(inputs, prior, gate_in, gate_state):
    gx = jnp.dot(inputs, gate_in, preferred_element_type=jnp.float32)
    gh = jnp.dot(prior, gate_state, preferred_element_type=jnp.float32)
    width = prior.shape[-1]
    reset = jax.nn.sigmoid(gx[:, :width] + gh[:, :width])
    update = jax.nn.sigmoid(gx[:, width : 2 * width] + gh[:, width : 2 * width])
    cand = jnp.tanh(gx[:, 2 * width :] + reset * gh[:, 2 * width :])
    return (1.0 - update) * cand + update * prior.astype(jnp.float32)


def per_device(
    states,
    row_of_user,
    event_users,
    event_features,
    feature_table,
    gate_in,
    gate_state,
    tower_in,
    tower_out,
):
    shards = lax.axis_size(AXES)
    events = event_users.shape[0]
    row_count, width = states.shape
    cap = 2 * (events // shards)
    rows = row_of_user[event_users]
    target = rows // row_count
    local = rows - target * row_count
    hits = (target[:, None] == jnp.arange(shards, dtype=jnp.int32)[None, :]).astype(jnp.int32)
    rank = jnp.sum((jnp.cumsum(hits, axis=0) - hits) * hits, axis=1)
    slot = target * cap + rank
    packed = local + row_count * event_features
    requests = jnp.full((shards * cap,), -1, jnp.int32).at[slot].set(packed).reshape(shards, cap)
    asked = lax.all_to_all(requests, AXES, split_axis=0, concat_axis=0, tiled=True).reshape(-1)
    valid = asked >= 0
    owned = jnp.where(valid, asked, 0)
    owned_feature = owned // row_count
    owned_row = owned - owned_feature * row_count
    prior = states[owned_row].astype(jnp.bfloat16)
    inputs = feature_table[owned_feature]
    fresh = gru_cell(inputs, prior, gate_in, gate_state)
    delta = fresh - prior.astype(jnp.float32)
    ids = jnp.where(valid, owned_row, row_count)
    total = jax.ops.segment_sum(delta, ids, num_segments=row_count + 1)[:row_count]
    count = jax.ops.segment_sum(valid.astype(jnp.int32), ids, num_segments=row_count + 1)[:row_count]
    new_states = states + total / jnp.maximum(count, 1).astype(jnp.float32)[:, None]
    joined = jnp.concatenate([fresh.astype(jnp.bfloat16), inputs], axis=1)
    hidden = jax.nn.gelu(
        lax.dot_general(
            joined,
            lax.all_gather(tower_in, AXES, axis=0, tiled=True),
            (((1,), (1,)), ((), ())),
            preferred_element_type=jnp.float32,
        )
    ).astype(jnp.bfloat16)
    tower = lax.dot_general(
        hidden,
        lax.all_gather(tower_out, AXES, axis=0, tiled=True),
        (((1,), (1,)), ((), ())),
        preferred_element_type=jnp.float32,
    )
    scored = jnp.sum(tower * inputs.astype(jnp.float32), axis=1) / jnp.sqrt(jnp.float32(width))
    back = lax.all_to_all(scored.reshape(shards, cap), AXES, split_axis=0, concat_axis=0, tiled=True)
    return (new_states, back.reshape(-1)[slot])


def solution(mesh):
    placed = (
        P(AXES, None),
        P(),
        P(AXES),
        P(AXES),
        P(),
        P(),
        P(),
        P(AXES, None),
        P(AXES, None),
    )
    return jax.shard_map(
        per_device,
        mesh=mesh,
        in_specs=placed,
        out_specs=(P(AXES, None), P(AXES)),
        check_vma=False,
    )
```

time: 187 us -> 199 us (1.064)
  blocking collectives: 20.7 us -> 0 us
  waiting for transfers between devices: 60.9 us -> 78.5 us
  local copies, waits for them, and re-layouts: 31.1 us -> 38 us
  starting transfers between devices: 10.3 us -> 17 us
  matrix products: 16.6 us -> 22 us
  other arithmetic: 32.1 us -> 28.2 us
    all_gather x2, waiting for transfers between devices: 24.2 us -> 64.4 us  [the longest x1 63.7 us: per_device(): lax.all_gather(tower_in, AXES, axis=0, tiled=True)]
    all_to_all x2, waiting for transfers between devices: 35.2 us -> 12.7 us  [the longest x1 9.32 us: per_device(): lax.all_to_all(requests, AXES, split_axis=0, concat_axis=0, tiled=True)]
    all_to_all x1 -> x0, blocking collectives: 20.7 us -> none  [per_device(): lax.all_to_all(requests, ('owner', 'worker'), split_axis=0, concat_axis=0...]
    dot_general x1, matrix products: 11.4 us -> 18.4 us  [per_device(): lax.dot_general(hidden, lax.all_gather(tower_out, AXES, axis=0, tiled=Tru...]
    all_to_all x2, starting transfers between devices: 10.3 us -> 16.9 us  [the longest x1 11.5 us: per_device(): lax.all_to_all(requests, AXES, split_axis=0, concat_axis=0, tiled=True)]
    gather x4, local copies, waits for them, and re-layouts: 14.2 us -> 18.9 us  [the longest x2 8.05 us: per_device(): inputs = feature_table[owned_feature]]
    scatter x1 -> x0, other arithmetic: 4.43 us -> none  [per_device(): outgoing = jnp.zeros((shards * cap, width), jnp.float32).at[slot].set(del...]
    unnamed x12 -> x10, local copies, waits for them, and re-layouts: 6.96 us -> 7.27 us
  transfers between devices with their start and end apart: 4 -> 4, of which waited for: 3 -> 4; matrix products, arithmetic and copies ran while one was open for 36% -> 32% of each run, Pallas kernels for 0% -> 0%
where the time goes in v1:
time: 199 us; the launch traced here: 198 us
  waiting for transfers between devices  78.5 us (39%)
  local copies, waits for them, and re-layouts  38 us (19%)
  other arithmetic  28.2 us (14%)
  matrix products  22 us (11%)
  starting transfers between devices  17 us (9%)
  between operations  14.3 us (7%)
    all_gather x1, waiting for transfers between devices, per_device(): lax.all_gather(tower_in, AXES, axis=0, tiled=True)  63.7 us
    dot_general x1, matrix products, per_device(): lax.dot_general(hidden, lax.all_gather(tower_out, AXES, axis=0, tiled=Tru...  18.4 us
    all_to_all x1, starting transfers between devices, per_device(): lax.all_to_all(requests, AXES, split_axis=0, concat_axis=0, tiled=True)  11.5 us
    scatter-add x1, other arithmetic, per_device(): jax.ops.segment_sum(delta, ids, num_segments=row_count + 1)[:row_count]  9.98 us
    all_to_all x1, waiting for transfers between devices, per_device(): lax.all_to_all(requests, AXES, split_axis=0, concat_axis=0, tiled=True)  9.32 us
    gather x2, local copies, waits for them, and re-layouts, per_device(): inputs = feature_table[owned_feature]  8.05 us
    gather x1, local copies, waits for them, and re-layouts, per_device(): prior = states[owned_row].astype(jnp.bfloat16)  7.46 us
    unnamed x10, local copies, waits for them, and re-layouts  7.27 us
  transfers between devices with their start and end apart: 4, of which 4 were waited for; matrix products, arithmetic and copies ran while one was open for 32% of the time, Pallas kernels for 0%

profile of v1, /device:TPU:1, one launch (start us, length us, event | category | flops | bytes accessed | tf_op | source)
XLA Modules:
  0.0 198.0 jit_solution(6553455652774412179)
XLA Ops:
  7.2 0.0 copy-start
  7.2 0.0 copy-start.3
  7.2 0.0 all-gather.6.cloned.1.call-start
  7.2 0.7 all-gather.6.cloned.1.call-update
  7.9 0.0 all-gather.4.cloned.1.call-start
  8.0 0.7 all-gather.4.cloned.1.call-update
  8.7 0.7 compare_select_fusion.8
  9.4 6.5 %gather_fusion = s32[512]{0:T(512)S(1)} fusion(s32[262144]{0:T(1024)} %param.10, s32[1024]{0:T(1024)S(1)} %pad_clamp_fusion.1), kind=kCustom, calls=%fused_computation | custom fusion | bytes 6144 | tf_op jit(solution)/shard_map/gather | solution.py:34
  15.9 0.1 copy.15
  16.0 0.2 fusion.41
  16.3 0.0 copy-done.3
  16.4 0.2 fusion.40
  16.6 2.4 %scatter_custom_fusion = s32[1024]{0:T(1024)S(1)} fusion(s32[512]{0:T(512)S(1)} %bitcast.51, s32[512]{0:T(512)S(1)} %get-tuple-element.10, s32[]{:T(128)} %constant.20.clone.1), kind=kCustom, calls=%fused_computation.94 | custom fusion | bytes 4100 | tf_op jit(solution)/shard_map/scatter | solution.py:41
  19.1 0.7 all_to_all.10
  19.8 11.5 %all-to-all-start = ((s32[128,1,8]{2,1,0:T(1,128)}), s32[128,1,8]{2,1,0:T(1,128)S(1)}, u32[]{:S(2)}, u32[]{:S(2)}) async-start(s32[128,1,8]{2,1,0:T(1,128)} %bitcast.7), calls=%async_computation | async-start | bytes 131072 | tf_op jit(solution)/shard_map/all_to_all | solution.py:42
  31.3 9.3 %all-to-all-done = s32[128,1,8]{2,1,0:T(1,128)S(1)} async-done(((s32[128,1,8]{2,1,0:T(1,128)}), s32[128,1,8]{2,1,0:T(1,128)S(1)}, u32[]{:S(2)}, u32[]{:S(2)}) %all-to-all-start) | async-done | bytes 4128 | tf_op jit(solution)/shard_map/all_to_all | solution.py:42
  40.6 0.5 broadcast.392
  41.1 1.0 fusion.44
  42.1 0.1 reshape.233
  42.2 0.1 reshape.288
  42.4 6.7 %gather_fusion.1 = bf16[1024,512]{1,0:T(8,128)(2,1)S(1)} fusion(bf16[4096,512]{1,0:T(8,128)(2,1)} %param.13, s32[1024]{0:T(1024)S(1)} %broadcast_clamp_fusion.1), kind=kCustom, calls=%fused_computation.1 | custom fusion | bytes 2101248 | tf_op jit(solution)/shard_map/gather | solution.py:48
  49.1 1.3 copy.18
  50.5 7.5 %gather_fusion.2 = f32[1024,512]{1,0:T(8,128)} fusion(f32[2048,512]{1,0:T(8,128)} %param.9, s32[1024]{0:T(1024)S(1)} %broadcast_clamp_fusion), kind=kCustom, calls=%fused_computation.2 | custom fusion | bytes 4198400 | tf_op jit(solution)/shard_map/gather | solution.py:47
  57.9 6.1 %scatter_custom_fusion.2 = s32[2049]{0:T(1024)S(1)} fusion(s32[1024]{0:T(1024)S(1)} %bitcast.53, s32[1024]{0:T(1024)S(1)} %reshape.288, s32[]{:T(128)} %constant.21.clone.1), kind=kCustom, calls=%fused_computation.66 | custom fusion | flops 1024 | bytes 8200 | tf_op jit(solution)/shard_map/scatter-add | solution.py:53
  64.0 0.0 copy-done
  64.0 0.0 copy-start.1
  64.1 0.0 copy-start.2
  64.1 1.8 fusion.66
  65.9 0.0 copy-done.1
  65.9 0.4 copy-done.2
  66.2 1.8 fusion.61
  68.0 3.1 %fusion.64 = (bf16[1024,512]{1,0:T(8,128)(2,1)}, f32[1024,512]{1,0:T(8,128)}) fusion(f32[1024,512]{1,0:T(8,128)S(1)} %copy-done.1, f32[1024,1536]{1,0:T(8,128)S(1)} %fusion.61, f32[1024,1536]{1,0:T(8,128)S(1)} %fusion.66), kind=kLoop, calls=%fused_computation.106 | loop fusion | flops 8912896 | bytes 17825792 | tf_op jit(solution)/shard_map/convert_element_type | solution.py:55
  71.1 10.0 %scatter_custom_fusion.1 = f32[2049,512]{1,0:T(8,128)} fusion(s32[1024]{0:T(1024)S(1)} %bitcast.54, f32[]{:T(128)} %constant.19.clone.1, f32[1024,512]{1,0:T(8,128)} %get-tuple-element.5, f32[1024,512]{1,0:T(8,128)} %gather_fusion.2), kind=kCustom, calls=%fused_computation.21 | custom fusion | flops 2097152 | bytes 8390660 | tf_op jit(solution)/shard_map/scatter-add | solution.py:52
  81.1 0.7 all-gather.6.cloned.1.call-done
  81.8 6.9 %reshape.294 = bf16[512,4096]{1,0:T(8,128)(2,1)} reshape(bf16[128,4,4096]{2,1,0:T(4,128)(2,1)} %all-gather.6.cloned.1.call-done) | data formatting | bytes 8388608
  88.6 63.7 %all-gather.4.cloned.1.call-done = bf16[4096,1024]{1,0:T(8,128)(2,1)} async-done(((bf16[32,1024]{1,0:T(8,128)(2,1)}), bf16[4096,1024]{1,0:T(8,128)(2,1)}) %all-gather.4.cloned.1.call-update) | async-done | bytes 8388624 | tf_op jit(solution)/shard_map/all_gather | solution.py:59
  152.4 18.4 %multiply_reduce_fusion = f32[1024]{0:T(1024)S(1)} fusion(bf16[1024,512]{0,1:T(8,128)(2,1)} %copy.18, bf16[512,4096]{1,0:T(8,128)(2,1)} %reshape.294, bf16[4096,1024]{1,0:T(8,128)(2,1)} %all-gather.4.cloned.1.call-done, bf16[1024,512]{1,0:T(8,128)(2,1)S(1)} %gather_fusion.1, bf16[1024,512]{1,0:T(8,128)(2,1)} %get-tuple-element.4), kind=kOutput, calls=%fused_computation.42 | convolution fusion | flops 12928416768 | bytes 15732736 | tf_op jit(solution)/shard_map/dot_general | solution.py:64
  170.8 0.7 div.84
  171.5 5.4 %all-to-all-start.1 = ((f32[128,1,8]{2,1,0:T(1,128)}), f32[128,1,8]{2,1,0:T(1,128)S(1)}, u32[]{:S(2)}, u32[]{:S(2)}) async-start(f32[128,1,8]{2,1,0:T(1,128)} %bitcast.12), calls=%async_computation.1 | async-start | bytes 131072 | tf_op jit(solution)/shard_map/all_to_all | solution.py:71
  177.0 6.0 %fusion.10 = f32[2048,512]{1,0:T(8,128)} fusion(f32[2048,512]{1,0:T(8,128)} %param.9, f32[2049,512]{1,0:T(8,128)} %scatter_custom_fusion.1, f32[2048]{0:T(1024)S(1)} %fusion.45), kind=kLoop, calls=%fused_computation.18 | loop fusion | flops 2097152 | bytes 12591104 | tf_op jit(solution)/shard_map/add | solution.py:54
  182.9 3.4 %all-to-all-done.1 = f32[128,1,8]{2,1,0:T(1,128)S(1)} async-done(((f32[128,1,8]{2,1,0:T(1,128)}), f32[128,1,8]{2,1,0:T(1,128)S(1)}, u32[]{:S(2)}, u32[]{:S(2)}) %all-to-all-start.1) | async-done | bytes 4128 | tf_op jit(solution)/shard_map/all_to_all | solution.py:71
  186.4 0.5 broadcast.393
  186.9 0.8 reduce.11
  187.7 0.1 reshape.234
  187.8 3.4 %gather_fusion.3 = f32[512]{0:T(512)} fusion(f32[1024]{0:T(1024)S(1)} %reshape.234, s32[1024]{0:T(1024)S(1)} %pad_clamp_fusion), kind=kCustom, calls=%fused_computation.3 | custom fusion | bytes 6144 | tf_op jit(solution)/shard_map/gather | solution.py:72
  (17 shorter events, 0.2 us)
Async XLA Ops:
  7.2 56.9 %copy-start = (bf16[512,1536]{1,0:T(8,128)(2,1)S(1)}, bf16[512,1536]{1,0:T(8,128)(2,1)}, u32[]{:S(2)}) copy-start(bf16[512,1536]{1,0:T(8,128)(2,1)} %param.14) | copy-start | bytes 4718596
  7.2 9.1 %copy-start.3 = (s32[512]{0:T(512)S(1)}, s32[512]{0:T(512)}, u32[]{:S(2)}) copy-start(s32[512]{0:T(512)} %param.12) | copy-start | bytes 6148
  7.2 74.6 %all-gather.6.cloned.1.call-start = ((), (), s32[]{:S(2)}) async-start(), calls=%async_computation.3 | async-start | bytes 4227072 | tf_op jit(solution)/shard_map/all_gather | solution.py:66
  7.9 144.5 %all-gather.4.cloned.1.call-start = ((), (), s32[]{:S(2)}) async-start(), calls=%async_computation.2 | async-start | bytes 8454144 | tf_op jit(solution)/shard_map/all_gather | solution.py:59
  19.8 20.8 %all-to-all-start = ((s32[128,1,8]{2,1,0:T(1,128)}), s32[128,1,8]{2,1,0:T(1,128)S(1)}, u32[]{:S(2)}, u32[]{:S(2)}) async-start(s32[128,1,8]{2,1,0:T(1,128)} %bitcast.7), calls=%async_computation | async-start | bytes 131072 | tf_op jit(solution)/shard_map/all_to_all | solution.py:42
  64.0 1.8 copy-start.1
  64.1 2.2 %copy-start.2 = (bf16[512,1536]{1,0:T(8,128)(2,1)S(1)}, bf16[512,1536]{1,0:T(8,128)(2,1)}, u32[]{:S(2)}) copy-start(bf16[512,1536]{1,0:T(8,128)(2,1)} %param.15) | copy-start | bytes 4718596
  171.5 14.8 %all-to-all-start.1 = ((f32[128,1,8]{2,1,0:T(1,128)}), f32[128,1,8]{2,1,0:T(1,128)S(1)}, u32[]{:S(2)}, u32[]{:S(2)}) async-start(f32[128,1,8]{2,1,0:T(1,128)} %bitcast.12), calls=%async_computation.1 | async-start | bytes 131072 | tf_op jit(solution)/shard_map/all_to_all | solution.py:71
Sparse Core Ops, SparseCore 0:
  11.2 70.5 all-gather.5
  84.7 67.5 all-gather.3

commit v2 on v1

v2 whole, which is shorter than its diff:
```python
import functools

import jax
import jax.numpy as jnp
from jax import lax
from jax.experimental import pallas as pl
from jax.experimental.pallas import tpu as pltpu
from jax.sharding import PartitionSpec as P

AXES = ("owner", "worker")
MESH = pl.DeviceIdType.MESH
RING = 4
NDEV = 128
CAP = 8
F32 = jnp.float32
BF16 = jnp.bfloat16


def iota(shape, dim):
    return lax.broadcasted_iota(jnp.int32, shape, dim)


def one_hot(hit):
    return jnp.where(hit, 1.0, 0.0).astype(BF16)


def dot(a, b):
    return jnp.dot(a, b, preferred_element_type=F32)


def dot_nt(a, b):
    return lax.dot_general(a, b, (((1,), (1,)), ((), ())), preferred_element_type=F32)


def kernel(
    ids_ref,
    table_ref,
    states_ref,
    features_ref,
    gate_in_ref,
    gate_state_ref,
    tin_ref,
    tout_ref,
    new_ref,
    score_ref,
    table,
    st,
    st16,
    feat,
    gin,
    gst,
    win,
    wout,
    raw,
    qsend,
    qrecv,
    ssend,
    srecv,
    hits,
    ranks,
    locb,
    featb,
    locr,
    joined,
    prior,
    xperm,
    dl,
    perm,
    acc,
    load_sem,
    own_sem,
    out_sem,
    a2a_sem,
    send1,
    recv1,
    send2,
    recv2,
    send3,
    recv3,
    sib_send,
    sib_recv,
):
    y = lax.axis_index("owner")
    w = lax.axis_index("worker")
    x, z, c = w // 8, (w // 2) % RING, w % 2
    me = y * 32 + w
    pos = {"x": x, "y": y, "z": z}

    def device(axis, p):
        at = dict(pos)
        at[axis] = p
        return (at["y"], at["x"] * 8 + at["z"] * 2 + c)

    sibling = (y, x * 8 + z * 2 + (1 - c))

    def remote(ref, send, recv, to, dst=None):
        return pltpu.make_async_remote_copy(
            src_ref=ref,
            dst_ref=ref if dst is None else dst,
            send_sem=send,
            recv_sem=recv,
            device_id=to,
            device_id_type=MESH,
        )

    loads = [
        pltpu.make_async_copy(src, dst, load_sem.at[i])
        for i, (src, dst) in enumerate(
            (
                (table_ref, table),
                (states_ref, st),
                (features_ref, feat),
                (gate_in_ref, gin),
                (gate_state_ref, gst),
            )
        )
    ]
    own = [
        pltpu.make_async_copy(tout_ref, raw.at[z], own_sem.at[0]),
        pltpu.make_async_copy(tin_ref.at[pl.ds(0, 16)], win.at[y, x, z, c, 0], own_sem.at[1]),
        pltpu.make_async_copy(tin_ref.at[pl.ds(16, 16)], win.at[y, x, z, c, 1], own_sem.at[2]),
    ]
    loads[0].start()

    firsts = (
        ("z", tout_ref, raw.at[z]),
        ("x", tin_ref.at[pl.ds(0, 16)], win.at[y, x, z, c, 0]),
        ("y", tin_ref.at[pl.ds(16, 16)], win.at[y, x, z, c, 1]),
    )
    stage1 = []
    for part, (axis, src, dst) in enumerate(firsts):
        for hop in (1, 3, 2):
            stage1.append(
                remote(
                    src,
                    send1.at[part, hop - 1],
                    recv1.at[part, hop - 1],
                    device(axis, (pos[axis] + hop) % RING),
                    dst,
                )
            )
    for copy in stage1:
        copy.start()
    for copy in own:
        copy.start()
    for copy in loads[1:]:
        copy.start()

    def view2(part, p, h):
        if part == 0:
            return wout.at[y, p, c, :, pl.ds(2048 * h, 2048)]
        if part == 1:
            return win.at[p, pl.ds(2 * h, 2), z, c, 0]
        return win.at[pl.ds(2 * h, 2), x, p, c, 1]

    def view3(part, p, h):
        if part == 0:
            return wout.at[p, pl.ds(2 * h, 2), c]
        if part == 1:
            return win.at[pl.ds(2 * h, 2), :, p, c, 0]
        return win.at[pl.ds(2 * h, 2), p, :, c, 1]

    class Ring:
        def __init__(self, view, axis, part, send, recv):
            p = pos[axis]
            up, down, far = (p + 1) % RING, (p + RING - 1) % RING, (p + 2) % RING
            right, left = device(axis, up), device(axis, down)

            def hop(n, block, h, to):
                return remote(view(part, block, h), send.at[part, n], recv.at[part, n], to)

            self.sends = [
                hop(0, p, 0, right),
                hop(1, p, 1, left),
                hop(2, p, 1, right),
                hop(3, p, 0, left),
                hop(4, down, 0, right),
                hop(5, up, 1, left),
            ]
            self.arrivals = [
                hop(0, down, 0, right),
                hop(1, up, 1, left),
                hop(2, down, 1, right),
                hop(3, up, 0, left),
                hop(4, far, 0, right),
                hop(5, far, 1, left),
            ]

        def begin(self):
            for n in range(4):
                self.sends[n].start()

        def forward(self):
            for n in (0, 1):
                self.arrivals[n].wait_recv()
                self.sends[4 + n].start()

        def arrive(self, *which):
            for n in which:
                self.arrivals[n].wait_recv()

        def drain(self):
            for copy in self.sends:
                copy.wait_send()

    ids = ids_ref[...].astype(F32)
    both = jnp.where(
        iota((128, 512), 0) < 64,
        jnp.broadcast_to(ids[0:1], (128, 512)),
        jnp.broadcast_to(ids[1:2], (128, 512)),
    )
    both = both.T
    user = both[:, 0:1].astype(jnp.int32)
    feature = both[:, 64:65].astype(jnp.int32)
    user_b = jnp.broadcast_to(user, (512, 128))
    lanes = iota((512, 128), 1)
    loads[0].wait()
    rows3 = jnp.zeros((512, 384), F32)
    for k in range(4):
        piece = table[pl.ds(512 * k, 512), :]
        parts = [piece & 255, (piece >> 8) & 255, piece >> 16]
        bytes3 = jnp.concatenate([v.astype(F32).astype(BF16) for v in parts], axis=1)
        pick = one_hot(iota((512, 512), 1) + 512 * k == (user >> 7))
        rows3 = rows3 + dot(pick, bytes3)
    found = rows3[:, 0:128] + 256.0 * rows3[:, 128:256] + 65536.0 * rows3[:, 256:384]
    row = jnp.sum(jnp.where(lanes == (user_b & 127), found, 0.0), axis=1, keepdims=True)
    row = row.astype(jnp.int32)
    hit = lanes == (row >> 11)
    hit16 = one_hot(hit)
    hits[...] = hit16
    before = one_hot(iota((512, 512), 1) < iota((512, 512), 0))
    rank = jnp.sum(jnp.where(hit, dot(before, hit16), 0.0), axis=1, keepdims=True)
    rank_b = jnp.broadcast_to(rank.astype(jnp.int32), (512, 128))
    ranks[...] = rank_b
    local = (row & 2047) + 1
    part = lanes // CAP
    value = jnp.where(
        part == 0,
        local & 255,
        jnp.where(part == 1, local >> 8, jnp.where(part == 2, feature & 255, feature >> 8)),
    )
    value = jnp.where((lanes % CAP == rank_b) & (part < 4), value, 0).astype(F32).astype(BF16)
    requests = dot(jnp.where(hit, 1.0, 0.0).T.astype(BF16), value)
    requests = requests + 256.0 * pltpu.roll(requests, 128 - CAP, 1)

    def exchange(values, send_ref, recv_ref, n):
        send_ref[...] = values.reshape(NDEV, 1, 128)

        @pl.loop(1, NDEV)
        def _(s):
            to = lax.rem(me + s, NDEV)
            remote(
                send_ref.at[to],
                a2a_sem.at[n],
                a2a_sem.at[n + 1],
                (to // 32, lax.rem(to, 32)),
                recv_ref.at[me],
            ).start()

        recv_ref[me] = send_ref[me]

    def all_but_one(ref, n):
        return pltpu.make_async_copy(ref.at[pl.ds(0, NDEV - 1)], ref.at[pl.ds(0, NDEV - 1)], a2a_sem.at[n])

    exchange(requests, qsend, qrecv, 0)

    for copy in own:
        copy.wait()
    for copy in stage1:
        copy.wait_recv()
    wout[y, x, c] = jnp.concatenate([raw[i].astype(F32) for i in range(RING)], axis=0).astype(BF16)
    second = [
        Ring(view2, axis, part, send2, recv2) for part, axis in enumerate(("x", "y", "z"))
    ]
    for ring in second:
        ring.begin()

    loads[1].wait()
    for k in range(4):
        st16[pl.ds(512 * k, 512), :] = st[pl.ds(512 * k, 512), :].astype(BF16)
    o = iota((512, 512), 1)
    o = (o - (o & 31)) + ((o >> 2) & 3) * 8 + ((o >> 4) & 1) * 4 + (o & 3)
    perm[...] = one_hot(iota((512, 512), 0) == o)

    for ring in second:
        ring.forward()

    all_but_one(qrecv, 1).wait()
    asked = qrecv[...].reshape(NDEV, 128)
    for k in range(CAP):
        locb[k] = jnp.broadcast_to(asked[:, k : k + 1], (NDEV, 128))
        featb[k] = jnp.broadcast_to(asked[:, 16 + k : 17 + k], (NDEV, 128))
    flipped = asked.T
    for k in range(CAP):
        locr[:, k * 128 : (k + 1) * 128] = jnp.broadcast_to(flipped[k : k + 1], (8, 128))

    def take_prior(m):
        at = locb[pl.ds(4 * m, 4)].reshape(512, 128)[:, 0:1].astype(jnp.int32)
        pick = one_hot(iota((512, 2048), 1) + 1 == at)
        prior[pl.ds(pl.multiple_of(512 * m, 512), 512), :] = dot(pick, st16[...]).astype(BF16)

    def take_inputs(m):
        at = featb[pl.ds(4 * m, 4)].reshape(512, 128)[:, 0:1].astype(jnp.int32)
        pick = one_hot(iota((512, 4096), 1) == at)
        joined[pl.ds(pl.multiple_of(512 * m, 512), 512), 512:1024] = dot(pick, feat[...]).astype(BF16)

    @pl.loop(0, 2)
    def _(m):
        take_prior(m)

    for ring in second:
        ring.arrive(2, 3, 4, 5)
    third = [Ring(view3, axis, part, send3, recv3) for part, axis in enumerate(("y", "z", "x"))]
    for ring in third:
        ring.begin()

    def to_sibling(part, axis, n):
        p = pos[axis]
        block = (p, (p + RING - 1) % RING, (p + 1) % RING, (p + 2) % RING)[n]
        if part == 0:
            ref = wout.at[block, :, c]
        elif part == 1:
            ref = win.at[:, :, block, c, 0]
        else:
            ref = win.at[:, block, :, c, 1]
        return remote(ref, sib_send.at[part, n], sib_recv.at[part, n], sibling)

    lasts = [[to_sibling(part, axis, n) for n in range(4)] for part, axis in enumerate(("y", "z", "x"))]
    for part in range(3):
        lasts[part][0].start()

    loads[2].wait()

    @pl.loop(0, 2)
    def _(m):
        take_inputs(m)

    for ring in third:
        ring.forward()

    loads[3].wait()
    loads[4].wait()

    @pl.loop(0, 4)
    def _(m):
        at = pl.ds(pl.multiple_of(256 * m, 256), 256)
        inputs = joined[at, 512:1024]
        old = prior[at, :]
        gx = dot(inputs, gin[...])
        gh = dot(old, gst[...])
        reset = 0.5 * jnp.tanh(0.5 * (gx[:, 0:512] + gh[:, 0:512])) + 0.5
        update = 0.5 * jnp.tanh(0.5 * (gx[:, 512:1024] + gh[:, 512:1024])) + 0.5
        cand = jnp.tanh(gx[:, 1024:1536] + reset * gh[:, 1024:1536])
        before = old.astype(F32)
        fresh = (1.0 - update) * cand + update * before
        joined[at, 0:512] = fresh.astype(BF16)
        delta = fresh - before
        high = delta.astype(BF16)
        dl[at, 0:512] = high
        dl[at, 512:1024] = (delta - high.astype(F32)).astype(BF16)
        xperm[at, :] = dot(inputs, perm[...]).astype(BF16)

    for part in range(3):
        third[part].arrive(2, 3)
        lasts[part][1].start()
        lasts[part][2].start()

    @pl.loop(0, 4)
    def _(m):
        at = pl.ds(pl.multiple_of(512 * m, 512), 512)
        owned = jnp.broadcast_to(locr[0:1, :], (512, 1024)).astype(jnp.int32)
        mine = iota((512, 1024), 0) + (512 * m + 1) == owned
        total2 = dot(one_hot(mine), dl[...])
        count = jnp.sum(jnp.where(mine, 1.0, 0.0), axis=1, keepdims=True)
        total = total2[:, 0:512] + total2[:, 512:1024]
        st[at, :] = st[at, :] + total / jnp.maximum(count, 1.0)

    result = pltpu.make_async_copy(st, new_ref, out_sem)
    result.start()

    for part in range(3):
        third[part].arrive(4, 5)
        lasts[part][3].start()
    for part in range(3):
        for copy in lasts[part]:
            copy.wait_recv()

    acc[...] = jnp.zeros_like(acc)

    @pl.loop(0, 16)
    def _(j):
        hid = pl.ds(pl.multiple_of(256 * j, 256), 256)
        first = win[j // RING, lax.rem(j, RING)].reshape(256, 1024)
        second_w = wout[:, :, :, :, hid].reshape(512, 256)

        @pl.loop(0, 2)
        def _(m):
            at = pl.ds(pl.multiple_of(512 * m, 512), 512)
            v = dot_nt(joined[at, :], first)
            inner = 0.7978845608028654 * (v + 0.044715 * (v * v * v))
            hidden = (v * (0.5 * (1.0 + jnp.tanh(inner)))).astype(BF16).astype(F32)
            prod = hidden * dot(xperm[at, :], second_w)
            acc[at, :] += prod[:, 0:128] + prod[:, 128:256]

    lane = iota((NDEV, 128), 1)
    scores = jnp.zeros((NDEV, 128), F32)
    for k in range(CAP):
        s = jnp.sum(acc[k * 128 : (k + 1) * 128, :], axis=1, keepdims=True)
        scores = jnp.where(lane == k, s, scores)
    scores = scores * (1.0 / (512.0**0.5))
    exchange(scores, ssend, srecv, 2)

    for copy in stage1:
        copy.wait_send()
    for ring in second + third:
        ring.drain()
    for part in range(3):
        for copy in lasts[part]:
            copy.wait_send()
    all_but_one(qsend, 0).wait()
    result.wait()

    all_but_one(srecv, 3).wait()
    back = srecv[...].reshape(NDEV, 128)
    high = back.astype(BF16)
    rest = back - high.astype(F32)
    middle = rest.astype(BF16)
    low = (rest - middle.astype(F32)).astype(BF16)
    three = jnp.concatenate([high, middle, low], axis=1)
    got = dot(hits[...], three)
    got = got[:, 0:128] + got[:, 128:256] + got[:, 256:384]
    picked = jnp.where(iota((512, 128), 1) == ranks[...], got, 0.0)
    score = jnp.sum(picked, axis=1, keepdims=True)
    score_ref[...] = jnp.broadcast_to(score, (512, 128)).T[0:1, :]
    all_but_one(ssend, 2).wait()


def per_device(
    states,
    row_of_user,
    event_users,
    event_features,
    feature_table,
    gate_in,
    gate_state,
    tower_in,
    tower_out,
):
    ids = jnp.stack([event_users, event_features])
    table = row_of_user.reshape(2048, 128)
    anywhere = pl.BlockSpec(memory_space=pl.ANY)
    vmem = pl.BlockSpec(memory_space=pltpu.VMEM)
    dma = pltpu.SemaphoreType.DMA
    new_states, scores = pl.pallas_call(
        kernel,
        out_shape=(
            jax.ShapeDtypeStruct((2048, 512), F32),
            jax.ShapeDtypeStruct((1, 512), F32),
        ),
        in_specs=[vmem] + [anywhere] * 7,
        out_specs=(anywhere, vmem),
        scratch_shapes=[
            pltpu.VMEM((2048, 128), jnp.int32),
            pltpu.VMEM((2048, 512), F32),
            pltpu.VMEM((2048, 512), BF16),
            pltpu.VMEM((4096, 512), BF16),
            pltpu.VMEM((512, 1536), BF16),
            pltpu.VMEM((512, 1536), BF16),
            pltpu.VMEM((4, 4, 4, 2, 2, 16, 1024), BF16),
            pltpu.VMEM((4, 4, 2, 16, 4096), BF16),
            pltpu.VMEM((4, 4, 4096), BF16),
            pltpu.VMEM((128, 1, 128), F32),
            pltpu.VMEM((128, 1, 128), F32),
            pltpu.VMEM((128, 1, 128), F32),
            pltpu.VMEM((128, 1, 128), F32),
            pltpu.VMEM((512, 128), BF16),
            pltpu.VMEM((512, 128), jnp.int32),
            pltpu.VMEM((8, 128, 128), F32),
            pltpu.VMEM((8, 128, 128), F32),
            pltpu.VMEM((8, 1024), F32),
            pltpu.VMEM((1024, 1024), BF16),
            pltpu.VMEM((1024, 512), BF16),
            pltpu.VMEM((1024, 512), BF16),
            pltpu.VMEM((1024, 1024), BF16),
            pltpu.VMEM((512, 512), BF16),
            pltpu.VMEM((1024, 128), F32),
            dma((5,)),
            dma((3,)),
            dma,
            dma((4,)),
            dma((3, 3)),
            dma((3, 3)),
            dma((3, 6)),
            dma((3, 6)),
            dma((3, 6)),
            dma((3, 6)),
            dma((3, 4)),
            dma((3, 4)),
        ],
        compiler_params=pltpu.CompilerParams(has_side_effects=True, vmem_limit_bytes=60 * 1024 * 1024),
    )(ids, table, states, feature_table, gate_in, gate_state, tower_in, tower_out)
    return new_states, scores.reshape(512)


def solution(mesh):
    placed = (
        P(AXES, None),
        P(),
        P(AXES),
        P(AXES),
        P(),
        P(),
        P(),
        P(AXES, None),
        P(AXES, None),
    )
    return jax.shard_map(
        per_device,
        mesh=mesh,
        in_specs=placed,
        out_specs=(P(AXES, None), P(AXES)),
        check_vma=False,
    )
```

time: 199 us -> 93.1 us (0.47)
  Pallas kernels: 0 us -> 85.8 us
  waiting for transfers between devices: 78.5 us -> 0 us
  local copies, waits for them, and re-layouts: 38 us -> 5.22 us
  other arithmetic: 28.2 us -> 1.3 us
  matrix products: 22 us -> 0 us
  starting transfers between devices: 17 us -> 0 us
  between operations: 14.3 us -> 0.65 us
    pallas_call x0 -> x1, Pallas kernels: none -> 85.8 us  [per_device(): pl.pallas_call(kernel, out_shape=(jax.ShapeDtypeStruct((2048, 512), F32),...]
    all_gather x2 -> x0, waiting for transfers between devices: 64.4 us -> none  [the longest x1 63.7 us: per_device(): lax.all_gather(tower_in, AXES, axis=0, tiled=True)]
    gather x5 -> x0, local copies, waits for them, and re-layouts: 25.4 us -> none  [the longest x2 8.05 us: per_device(): inputs = feature_table[owned_feature]]
    dot_general x3 -> x0, matrix products: 22 us -> none  [the longest x1 18.4 us: per_device(): lax.dot_general(hidden, lax.all_gather(tower_out, AXES, axis=0, tiled=Tru...]
    all_to_all x2 -> x0, starting transfers between devices: 16.9 us -> none  [the longest x1 11.5 us: per_device(): lax.all_to_all(requests, AXES, split_axis=0, concat_axis=0, tiled=True)]
    scatter-add x2 -> x0, other arithmetic: 16.1 us -> none  [the longest x1 9.98 us: per_device(): jax.ops.segment_sum(delta, ids, num_segments=row_count + 1)[:row_count]]
    all_to_all x2 -> x0, waiting for transfers between devices: 12.7 us -> none  [the longest x1 9.32 us: per_device(): lax.all_to_all(requests, AXES, split_axis=0, concat_axis=0, tiled=True)]
    add x2 -> x0, other arithmetic: 5.99 us -> none  [the longest x1 5.98 us: per_device(): states + total / jnp.maximum(count, 1).astype(jnp.float32)[:, None]]
  transfers between devices with their start and end apart: 4 -> 0, of which waited for: 4 -> 0; matrix products, arithmetic and copies ran while one was open for 32% -> 0% of each run, Pallas kernels for 0% -> 0%
where the time goes in v2:
time: 93.1 us; the launch traced here: 92.9 us
  Pallas kernels  85.8 us (92%)
  local copies, waits for them, and re-layouts  5.22 us (6%)
  other arithmetic  1.3 us (1%)
    pallas_call x1, Pallas kernels, per_device(): pl.pallas_call(kernel, out_shape=(jax.ShapeDtypeStruct((2048, 512), F32),...  85.8 us
    unnamed x4, local copies, waits for them, and re-layouts  5.22 us

profile of v2, /device:TPU:1, one launch (start us, length us, event | category | flops | bytes accessed | tf_op | source)
XLA Modules:
  0.0 92.9 jit_solution(8469184496022347442)
XLA Ops:
  0.6 1.3 %pad_add_fusion.ids_ref = s32[2,512]{1,0:T(2,128)} fusion(s32[1,512]{1,0:T(1,128)} %bitcast.6, s32[1,512]{1,0:T(1,128)} %bitcast.7), kind=kLoop, calls=%fused_computation | loop fusion | flops 1024 | bytes 8192 | tf_op jit(solution)/shard_map/stack | solution.py:449
  1.9 85.8 %shard_map.104 = (f32[2048,512]{1,0:T(8,128)}, f32[1,512]{1,0:T(1,128)}) custom-call(s32[2,512]{1,0:T(2,128)} %pad_add_fusion.ids_ref, s32[2048,128]{1,0:T(8,128)} %bitcast.4, f32[2048,512]{1,0:T(8,128)} %states_ref.1, bf16[4096,512]{1,0:T(8,128)(2,1)} %features_ref.1, bf16[512,1536]{1,0:T(8,128)(2,1)} %gate_in_ref.1, bf16[512,1536]{1,0:T(8,128)(2,1)} %gate_state_ref.1, ...), custom_call_target="tpu_custom_call" | custom-call | tf_op jit(solution)/shard_map/pallas_call | solution.py:454
  87.7 0.0 copy-start
  87.7 4.6 %copy.13 = f32[2048,512]{1,0:T(8,128)} copy(f32[2048,512]{1,0:T(8,128)} %get-tuple-element.8) | data formatting | bytes 8388608
  92.4 0.0 copy-done
  92.4 0.6 copy.14
Async XLA Ops:
  87.7 4.7 %copy-start = (f32[1,512]{1,0:T(1,128)S(1)}, f32[1,512]{1,0:T(1,128)}, u32[]{:S(2)}) copy-start(f32[1,512]{1,0:T(1,128)} %get-tuple-element.5) | copy-start | bytes 6148

commit v3 on v2

--- a/solution.py
+++ b/solution.py
@@ -53,8 +53,10 @@
     wout,
     raw,
     qsend,
+    qmid,
     qrecv,
     ssend,
+    smid,
     srecv,
     hits,
     ranks,
@@ -66,6 +68,7 @@
     xperm,
     dl,
     perm,
+    hidden,
     acc,
     load_sem,
     own_sem,
@@ -83,8 +86,8 @@
     y = lax.axis_index("owner")
     w = lax.axis_index("worker")
     x, z, c = w // 8, (w // 2) % RING, w % 2
-    me = y * 32 + w
     pos = {"x": x, "y": y, "z": z}
+    yx, zc = y * RING + x, z * 2 + c
 
     def device(axis, p):
         at = dict(pos)
@@ -92,6 +95,12 @@
         return (at["y"], at["x"] * 8 + at["z"] * 2 + c)
 
     sibling = (y, x * 8 + z * 2 + (1 - c))
+
+    def to_plane(p):
+        return (p // RING, lax.rem(p, RING) * 8 + zc)
+
+    def to_row(p):
+        return (y, x * 8 + p)
 
     def remote(ref, send, recv, to, dst=None):
         return pltpu.make_async_remote_copy(
@@ -120,7 +129,18 @@
         pltpu.make_async_copy(tin_ref.at[pl.ds(0, 16)], win.at[y, x, z, c, 0], own_sem.at[1]),
         pltpu.make_async_copy(tin_ref.at[pl.ds(16, 16)], win.at[y, x, z, c, 1], own_sem.at[2]),
     ]
-    loads[0].start()
+    for copy in loads + own:
+        copy.start()
+
+    entry = pltpu.get_barrier_semaphore()
+
+    @pl.loop(1, 16)
+    def _(s):
+        pl.semaphore_signal(entry, 1, device_id=to_plane(lax.rem(yx + s, 16)), device_id_type=MESH)
+
+    @pl.loop(1, 8)
+    def _(s):
+        pl.semaphore_signal(entry, 1, device_id=to_row(lax.rem(zc + s, 8)), device_id_type=MESH)
 
     firsts = (
         ("z", tout_ref, raw.at[z]),
@@ -139,19 +159,16 @@
                     dst,
                 )
             )
+    pl.semaphore_wait(entry, 22)
     for copy in stage1:
         copy.start()
-    for copy in own:
-        copy.start()
-    for copy in loads[1:]:
-        copy.start()
-
-    def view2(part, p, h):
-        if part == 0:
-            return wout.at[y, p, c, :, pl.ds(2048 * h, 2048)]
-        if part == 1:
-            return win.at[p, pl.ds(2 * h, 2), z, c, 0]
-        return win.at[pl.ds(2 * h, 2), x, p, c, 1]
+
+    stage2 = []
+    for part, axis in enumerate(("x", "y", "z")):
+        block = (wout.at[y, x, c], win.at[y, :, z, c, 0], win.at[:, x, z, c, 1])[part]
+        for hop in (1, 3, 2):
+            to = device(axis, (pos[axis] + hop) % RING)
+            stage2.append(remote(block, send2.at[part, hop - 1], recv2.at[part, hop - 1], to))
 
     def view3(part, p, h):
         if part == 0:
@@ -225,6 +242,14 @@
     found = rows3[:, 0:128] + 256.0 * rows3[:, 128:256] + 65536.0 * rows3[:, 256:384]
     row = jnp.sum(jnp.where(lanes == (user_b & 127), found, 0.0), axis=1, keepdims=True)
     row = row.astype(jnp.int32)
+    for copy in own:
+        copy.wait()
+    for copy in stage1:
+        copy.wait_recv()
+    wout[y, x, c] = jnp.concatenate([raw[i].astype(F32) for i in range(RING)], axis=0).astype(BF16)
+    for copy in stage2:
+        copy.start()
+
     hit = lanes == (row >> 11)
     hit16 = one_hot(hit)
     hits[...] = hit16
@@ -243,37 +268,19 @@
     requests = dot(jnp.where(hit, 1.0, 0.0).T.astype(BF16), value)
     requests = requests + 256.0 * pltpu.roll(requests, 128 - CAP, 1)
 
-    def exchange(values, send_ref, recv_ref, n):
-        send_ref[...] = values.reshape(NDEV, 1, 128)
-
-        @pl.loop(1, NDEV)
+    def spread(src, dst, mine, count, n, to):
+        @pl.loop(1, count)
         def _(s):
-            to = lax.rem(me + s, NDEV)
-            remote(
-                send_ref.at[to],
-                a2a_sem.at[n],
-                a2a_sem.at[n + 1],
-                (to // 32, lax.rem(to, 32)),
-                recv_ref.at[me],
-            ).start()
-
-        recv_ref[me] = send_ref[me]
-
-    def all_but_one(ref, n):
-        return pltpu.make_async_copy(ref.at[pl.ds(0, NDEV - 1)], ref.at[pl.ds(0, NDEV - 1)], a2a_sem.at[n])
-
-    exchange(requests, qsend, qrecv, 0)
-
-    for copy in own:
-        copy.wait()
-    for copy in stage1:
-        copy.wait_recv()
-    wout[y, x, c] = jnp.concatenate([raw[i].astype(F32) for i in range(RING)], axis=0).astype(BF16)
-    second = [
-        Ring(view2, axis, part, send2, recv2) for part, axis in enumerate(("x", "y", "z"))
-    ]
-    for ring in second:
-        ring.begin()
+            p = lax.rem(mine + s, count)
+            remote(src(p), a2a_sem.at[n], a2a_sem.at[n + 1], to(p), dst.at[mine]).start()
+
+    def settle(ref, count, n):
+        block = ref.at[pl.ds(0, count - 1)]
+        pltpu.make_async_copy(block, block, a2a_sem.at[n]).wait()
+
+    qsend[...] = requests.reshape(16, 8, 1, 128)
+    spread(lambda p: qsend.at[p], qmid, yx, 16, 0, to_plane)
+    qmid[yx] = qsend[yx]
 
     loads[1].wait()
     for k in range(4):
@@ -282,34 +289,12 @@
     o = (o - (o & 31)) + ((o >> 2) & 3) * 8 + ((o >> 4) & 1) * 4 + (o & 3)
     perm[...] = one_hot(iota((512, 512), 0) == o)
 
-    for ring in second:
-        ring.forward()
-
-    all_but_one(qrecv, 1).wait()
-    asked = qrecv[...].reshape(NDEV, 128)
-    for k in range(CAP):
-        locb[k] = jnp.broadcast_to(asked[:, k : k + 1], (NDEV, 128))
-        featb[k] = jnp.broadcast_to(asked[:, 16 + k : 17 + k], (NDEV, 128))
-    flipped = asked.T
-    for k in range(CAP):
-        locr[:, k * 128 : (k + 1) * 128] = jnp.broadcast_to(flipped[k : k + 1], (8, 128))
-
-    def take_prior(m):
-        at = locb[pl.ds(4 * m, 4)].reshape(512, 128)[:, 0:1].astype(jnp.int32)
-        pick = one_hot(iota((512, 2048), 1) + 1 == at)
-        prior[pl.ds(pl.multiple_of(512 * m, 512), 512), :] = dot(pick, st16[...]).astype(BF16)
-
-    def take_inputs(m):
-        at = featb[pl.ds(4 * m, 4)].reshape(512, 128)[:, 0:1].astype(jnp.int32)
-        pick = one_hot(iota((512, 4096), 1) == at)
-        joined[pl.ds(pl.multiple_of(512 * m, 512), 512), 512:1024] = dot(pick, feat[...]).astype(BF16)
-
-    @pl.loop(0, 2)
-    def _(m):
-        take_prior(m)
-
-    for ring in second:
-        ring.arrive(2, 3, 4, 5)
+    settle(qmid, 16, 1)
+    spread(lambda p: qmid.at[:, p], qrecv, zc, 8, 2, to_row)
+    qrecv[zc] = qmid[:, zc]
+
+    for copy in stage2:
+        copy.wait_recv()
     third = [Ring(view3, axis, part, send3, recv3) for part, axis in enumerate(("y", "z", "x"))]
     for ring in third:
         ring.begin()
@@ -329,17 +314,43 @@
     for part in range(3):
         lasts[part][0].start()
 
-    loads[2].wait()
+    settle(qrecv, 8, 3)
+    asked = qrecv[...].reshape(NDEV, 128)
+    for k in range(CAP):
+        locb[k] = jnp.broadcast_to(asked[:, k : k + 1], (NDEV, 128))
+        featb[k] = jnp.broadcast_to(asked[:, 16 + k : 17 + k], (NDEV, 128))
+    flipped = asked.T
+    for k in range(CAP):
+        locr[:, k * 128 : (k + 1) * 128] = jnp.broadcast_to(flipped[k : k + 1], (8, 128))
+
+    def take_prior(m):
+        at = locb[pl.ds(4 * m, 4)].reshape(512, 128)[:, 0:1].astype(jnp.int32)
+        pick = one_hot(iota((512, 2048), 1) + 1 == at)
+        prior[pl.ds(pl.multiple_of(512 * m, 512), 512), :] = dot(pick, st16[...]).astype(BF16)
+
+    def take_inputs(m):
+        at = featb[pl.ds(4 * m, 4)].reshape(512, 128)[:, 0:1].astype(jnp.int32)
+        pick = one_hot(iota((512, 4096), 1) == at)
+        joined[pl.ds(pl.multiple_of(512 * m, 512), 512), 512:1024] = dot(pick, feat[...]).astype(BF16)
+
+    @pl.loop(0, 2)
+    def _(m):
+        take_prior(m)
+
+    for ring in third:
+        ring.forward()
+
+    for copy in loads[2:]:
+        copy.wait()
 
     @pl.loop(0, 2)
     def _(m):
         take_inputs(m)
 
-    for ring in third:
-        ring.forward()
-
-    loads[3].wait()
-    loads[4].wait()
+    for part in range(3):
+        third[part].arrive(2, 3)
+        lasts[part][1].start()
+        lasts[part][2].start()
 
     @pl.loop(0, 4)
     def _(m):
@@ -361,12 +372,10 @@
         xperm[at, :] = dot(inputs, perm[...]).astype(BF16)
 
     for part in range(3):
-        third[part].arrive(2, 3)
-        lasts[part][1].start()
-        lasts[part][2].start()
-
-    @pl.loop(0, 4)
-    def _(m):
+        third[part].arrive(4, 5)
+        lasts[part][3].start()
+
+    def update(m):
         at = pl.ds(pl.multiple_of(512 * m, 512), 512)
         owned = jnp.broadcast_to(locr[0:1, :], (512, 1024)).astype(jnp.int32)
         mine = iota((512, 1024), 0) + (512 * m + 1) == owned
@@ -375,52 +384,61 @@
         total = total2[:, 0:512] + total2[:, 512:1024]
         st[at, :] = st[at, :] + total / jnp.maximum(count, 1.0)
 
-    result = pltpu.make_async_copy(st, new_ref, out_sem)
-    result.start()
-
-    for part in range(3):
-        third[part].arrive(4, 5)
-        lasts[part][3].start()
+    @pl.loop(0, 2)
+    def _(m):
+        update(m)
+
     for part in range(3):
         for copy in lasts[part]:
             copy.wait_recv()
-
-    acc[...] = jnp.zeros_like(acc)
 
     @pl.loop(0, 16)
     def _(j):
         hid = pl.ds(pl.multiple_of(256 * j, 256), 256)
         first = win[j // RING, lax.rem(j, RING)].reshape(256, 1024)
-        second_w = wout[:, :, :, :, hid].reshape(512, 256)
-
-        @pl.loop(0, 2)
-        def _(m):
-            at = pl.ds(pl.multiple_of(512 * m, 512), 512)
+        for m in range(2):
+            at = pl.ds(512 * m, 512)
             v = dot_nt(joined[at, :], first)
-            inner = 0.7978845608028654 * (v + 0.044715 * (v * v * v))
-            hidden = (v * (0.5 * (1.0 + jnp.tanh(inner)))).astype(BF16).astype(F32)
-            prod = hidden * dot(xperm[at, :], second_w)
-            acc[at, :] += prod[:, 0:128] + prod[:, 128:256]
+            inner = v * (0.7978845608028654 + 0.035677408136300125 * (v * v))
+            hidden[at, hid] = (v + v * jnp.tanh(inner)).astype(BF16)
+
+    @pl.loop(0, 4)
+    def _(m):
+        at = pl.ds(pl.multiple_of(256 * m, 256), 256)
+        tower = dot_nt(hidden[at, :], wout[...].reshape(512, 4096))
+        prod = tower * xperm[at, :].astype(F32)
+        acc[at, :] = (prod[:, 0:128] + prod[:, 128:256]) + (prod[:, 256:384] + prod[:, 384:512])
 
     lane = iota((NDEV, 128), 1)
     scores = jnp.zeros((NDEV, 128), F32)
     for k in range(CAP):
         s = jnp.sum(acc[k * 128 : (k + 1) * 128, :], axis=1, keepdims=True)
         scores = jnp.where(lane == k, s, scores)
-    scores = scores * (1.0 / (512.0**0.5))
-    exchange(scores, ssend, srecv, 2)
+    scores = scores * (0.5 / (512.0**0.5))
+    ssend[...] = scores.reshape(8, 16, 1, 128)
+    spread(lambda p: ssend.at[p], smid, zc, 8, 4, to_row)
+    smid[zc] = ssend[zc]
 
     for copy in stage1:
         copy.wait_send()
-    for ring in second + third:
+    for copy in stage2:
+        copy.wait_send()
+    for ring in third:
         ring.drain()
     for part in range(3):
         for copy in lasts[part]:
             copy.wait_send()
-    all_but_one(qsend, 0).wait()
-    result.wait()
-
-    all_but_one(srecv, 3).wait()
+    settle(qsend, 16, 0)
+    settle(qrecv, 8, 2)
+    update(2)
+    settle(smid, 8, 5)
+    spread(lambda p: smid.at[:, p], srecv, yx, 16, 6, to_plane)
+    srecv[yx] = smid[:, yx]
+    update(3)
+    result = pltpu.make_async_copy(st, new_ref, out_sem)
+    result.start()
+
+    settle(srecv, 16, 7)
     back = srecv[...].reshape(NDEV, 128)
     high = back.astype(BF16)
     rest = back - high.astype(F32)
@@ -432,7 +450,9 @@
     picked = jnp.where(iota((512, 128), 1) == ranks[...], got, 0.0)
     score = jnp.sum(picked, axis=1, keepdims=True)
     score_ref[...] = jnp.broadcast_to(score, (512, 128)).T[0:1, :]
-    all_but_one(ssend, 2).wait()
+    settle(ssend, 8, 4)
+    settle(srecv, 16, 6)
+    result.wait()
 
 
 def per_device(
@@ -469,10 +489,12 @@
             pltpu.VMEM((4, 4, 4, 2, 2, 16, 1024), BF16),
             pltpu.VMEM((4, 4, 2, 16, 4096), BF16),
             pltpu.VMEM((4, 4, 4096), BF16),
-            pltpu.VMEM((128, 1, 128), F32),
-            pltpu.VMEM((128, 1, 128), F32),
-            pltpu.VMEM((128, 1, 128), F32),
-            pltpu.VMEM((128, 1, 128), F32),
+            pltpu.VMEM((16, 8, 1, 128), F32),
+            pltpu.VMEM((16, 8, 1, 128), F32),
+            pltpu.VMEM((8, 16, 1, 128), F32),
+            pltpu.VMEM((8, 16, 1, 128), F32),
+            pltpu.VMEM((8, 16, 1, 128), F32),
+            pltpu.VMEM((16, 8, 1, 128), F32),
             pltpu.VMEM((512, 128), BF16),
             pltpu.VMEM((512, 128), jnp.int32),
             pltpu.VMEM((8, 128, 128), F32),
@@ -483,21 +505,24 @@
             pltpu.VMEM((1024, 512), BF16),
             pltpu.VMEM((1024, 1024), BF16),
             pltpu.VMEM((512, 512), BF16),
+            pltpu.VMEM((1024, 4096), BF16),
             pltpu.VMEM((1024, 128), F32),
             dma((5,)),
             dma((3,)),
             dma,
-            dma((4,)),
+            dma((8,)),
             dma((3, 3)),
             dma((3, 3)),
-            dma((3, 6)),
-            dma((3, 6)),
+            dma((3, 3)),
+            dma((3, 3)),
             dma((3, 6)),
             dma((3, 6)),
             dma((3, 4)),
             dma((3, 4)),
         ],
-        compiler_params=pltpu.CompilerParams(has_side_effects=True, vmem_limit_bytes=60 * 1024 * 1024),
+        compiler_params=pltpu.CompilerParams(
+            collective_id=0, has_side_effects=True, vmem_limit_bytes=60 * 1024 * 1024
+        ),
     )(ids, table, states, feature_table, gate_in, gate_state, tower_in, tower_out)
     return new_states, scores.reshape(512)
 

time: 93.1 us -> 81.1 us (0.87)
  Pallas kernels: 85.8 us -> 73.7 us
    pallas_call x1, Pallas kernels: 85.8 us -> 73.7 us  [per_device(): pl.pallas_call(kernel, out_shape=(jax.ShapeDtypeStruct((2048, 512), F32),...]
where the time goes in v3:
time: 81.1 us; the launch traced here: 80.9 us
  Pallas kernels  73.7 us (91%)
  local copies, waits for them, and re-layouts  5.22 us (6%)
  other arithmetic  1.3 us (2%)
    pallas_call x1, Pallas kernels, per_device(): pl.pallas_call(kernel, out_shape=(jax.ShapeDtypeStruct((2048, 512), F32),...  73.7 us
    unnamed x4, local copies, waits for them, and re-layouts  5.22 us

profile of v3, /device:TPU:1, one launch (start us, length us, event | category | flops | bytes accessed | tf_op | source)
XLA Modules:
  0.0 80.9 jit_solution(14653428257402871474)
XLA Ops:
  0.6 1.3 %pad_add_fusion.ids_ref = s32[2,512]{1,0:T(2,128)} fusion(s32[1,512]{1,0:T(1,128)} %bitcast.6, s32[1,512]{1,0:T(1,128)} %bitcast.7), kind=kLoop, calls=%fused_computation | loop fusion | flops 1024 | bytes 8192 | tf_op jit(solution)/shard_map/stack | solution.py:469
  1.9 73.7 %shard_map.104 = (f32[2048,512]{1,0:T(8,128)}, f32[1,512]{1,0:T(1,128)}) custom-call(s32[2,512]{1,0:T(2,128)} %pad_add_fusion.ids_ref, s32[2048,128]{1,0:T(8,128)} %bitcast.4, f32[2048,512]{1,0:T(8,128)} %states_ref.1, bf16[4096,512]{1,0:T(8,128)(2,1)} %features_ref.1, bf16[512,1536]{1,0:T(8,128)(2,1)} %gate_in_ref.1, bf16[512,1536]{1,0:T(8,128)(2,1)} %gate_state_ref.1, ...), custom_call_target="tpu_custom_call" | custom-call | tf_op jit(solution)/shard_map/pallas_call | solution.py:474
  75.7 0.0 copy-start
  75.7 4.6 %copy.13 = f32[2048,512]{1,0:T(8,128)} copy(f32[2048,512]{1,0:T(8,128)} %get-tuple-element.8) | data formatting | bytes 8388608
  80.3 0.0 copy-done
  80.3 0.6 copy.14
Async XLA Ops:
  75.7 4.7 %copy-start = (f32[1,512]{1,0:T(1,128)S(1)}, f32[1,512]{1,0:T(1,128)}, u32[]{:S(2)}) copy-start(f32[1,512]{1,0:T(1,128)} %get-tuple-element.5) | copy-start | bytes 6148

commit v4 on v3

--- a/solution.py
+++ b/solution.py
@@ -33,7 +33,8 @@
 
 
 def kernel(
-    ids_ref,
+    users_ref,
+    feats_ref,
     table_ref,
     states_ref,
     features_ref,
@@ -41,7 +42,8 @@
     gate_state_ref,
     tin_ref,
     tout_ref,
-    new_ref,
+    delta_ref,
+    slots_ref,
     score_ref,
     table,
     st,
@@ -125,7 +127,7 @@
         )
     ]
     own = [
-        pltpu.make_async_copy(tout_ref, raw.at[z], own_sem.at[0]),
+        pltpu.make_async_copy(tout_ref, raw.at[x], own_sem.at[0]),
         pltpu.make_async_copy(tin_ref.at[pl.ds(0, 16)], win.at[y, x, z, c, 0], own_sem.at[1]),
         pltpu.make_async_copy(tin_ref.at[pl.ds(16, 16)], win.at[y, x, z, c, 1], own_sem.at[2]),
     ]
@@ -143,8 +145,8 @@
         pl.semaphore_signal(entry, 1, device_id=to_row(lax.rem(zc + s, 8)), device_id_type=MESH)
 
     firsts = (
-        ("z", tout_ref, raw.at[z]),
-        ("x", tin_ref.at[pl.ds(0, 16)], win.at[y, x, z, c, 0]),
+        ("x", tout_ref, raw.at[x]),
+        ("z", tin_ref.at[pl.ds(0, 16)], win.at[y, x, z, c, 0]),
         ("y", tin_ref.at[pl.ds(16, 16)], win.at[y, x, z, c, 1]),
     )
     stage1 = []
@@ -159,22 +161,19 @@
                     dst,
                 )
             )
-    pl.semaphore_wait(entry, 22)
-    for copy in stage1:
-        copy.start()
 
     stage2 = []
-    for part, axis in enumerate(("x", "y", "z")):
-        block = (wout.at[y, x, c], win.at[y, :, z, c, 0], win.at[:, x, z, c, 1])[part]
+    for part, axis in enumerate(("y", "x", "z")):
+        block = (wout.at[y, z, c], win.at[y, x, :, c, 0], win.at[:, x, z, c, 1])[part]
         for hop in (1, 3, 2):
             to = device(axis, (pos[axis] + hop) % RING)
             stage2.append(remote(block, send2.at[part, hop - 1], recv2.at[part, hop - 1], to))
 
     def view3(part, p, h):
         if part == 0:
-            return wout.at[p, pl.ds(2 * h, 2), c]
+            return wout.at[pl.ds(2 * h, 2), p, c]
         if part == 1:
-            return win.at[pl.ds(2 * h, 2), :, p, c, 0]
+            return win.at[p, pl.ds(2 * h, 2), :, c, 0]
         return win.at[pl.ds(2 * h, 2), p, :, c, 1]
 
     class Ring:
@@ -220,11 +219,14 @@
             for copy in self.sends:
                 copy.wait_send()
 
-    ids = ids_ref[...].astype(F32)
+    pl.semaphore_wait(entry, 22)
+    for copy in stage1:
+        copy.start()
+
     both = jnp.where(
         iota((128, 512), 0) < 64,
-        jnp.broadcast_to(ids[0:1], (128, 512)),
-        jnp.broadcast_to(ids[1:2], (128, 512)),
+        jnp.broadcast_to(users_ref[...].astype(F32), (128, 512)),
+        jnp.broadcast_to(feats_ref[...].astype(F32), (128, 512)),
     )
     both = both.T
     user = both[:, 0:1].astype(jnp.int32)
@@ -242,14 +244,6 @@
     found = rows3[:, 0:128] + 256.0 * rows3[:, 128:256] + 65536.0 * rows3[:, 256:384]
     row = jnp.sum(jnp.where(lanes == (user_b & 127), found, 0.0), axis=1, keepdims=True)
     row = row.astype(jnp.int32)
-    for copy in own:
-        copy.wait()
-    for copy in stage1:
-        copy.wait_recv()
-    wout[y, x, c] = jnp.concatenate([raw[i].astype(F32) for i in range(RING)], axis=0).astype(BF16)
-    for copy in stage2:
-        copy.start()
-
     hit = lanes == (row >> 11)
     hit16 = one_hot(hit)
     hits[...] = hit16
@@ -282,11 +276,19 @@
     spread(lambda p: qsend.at[p], qmid, yx, 16, 0, to_plane)
     qmid[yx] = qsend[yx]
 
+    for copy in own:
+        copy.wait()
+    for copy in stage1:
+        copy.wait_recv()
+    wout[y, z, c] = jnp.concatenate([raw[i].astype(F32) for i in range(RING)], axis=0).astype(BF16)
+    for copy in stage2:
+        copy.start()
+
     loads[1].wait()
     for k in range(4):
         st16[pl.ds(512 * k, 512), :] = st[pl.ds(512 * k, 512), :].astype(BF16)
     o = iota((512, 512), 1)
-    o = (o - (o & 31)) + ((o >> 2) & 3) * 8 + ((o >> 4) & 1) * 4 + (o & 3)
+    o = (o - (o & 127)) + ((o >> 2) & 3) * 32 + ((o >> 5) & 3) * 8 + ((o >> 4) & 1) * 4 + (o & 3)
     perm[...] = one_hot(iota((512, 512), 0) == o)
 
     settle(qmid, 16, 1)
@@ -295,7 +297,7 @@
 
     for copy in stage2:
         copy.wait_recv()
-    third = [Ring(view3, axis, part, send3, recv3) for part, axis in enumerate(("y", "z", "x"))]
+    third = [Ring(view3, axis, part, send3, recv3) for part, axis in enumerate(("z", "y", "x"))]
     for ring in third:
         ring.begin()
 
@@ -303,14 +305,14 @@
         p = pos[axis]
         block = (p, (p + RING - 1) % RING, (p + 1) % RING, (p + 2) % RING)[n]
         if part == 0:
-            ref = wout.at[block, :, c]
+            ref = wout.at[:, block, c]
         elif part == 1:
-            ref = win.at[:, :, block, c, 0]
+            ref = win.at[block, :, :, c, 0]
         else:
             ref = win.at[:, block, :, c, 1]
         return remote(ref, sib_send.at[part, n], sib_recv.at[part, n], sibling)
 
-    lasts = [[to_sibling(part, axis, n) for n in range(4)] for part, axis in enumerate(("y", "z", "x"))]
+    lasts = [[to_sibling(part, axis, n) for n in range(4)] for part, axis in enumerate(("z", "y", "x"))]
     for part in range(3):
         lasts[part][0].start()
 
@@ -337,15 +339,14 @@
     def _(m):
         take_prior(m)
 
+    for copy in loads[2:]:
+        copy.wait()
+    take_inputs(0)
+
     for ring in third:
         ring.forward()
 
-    for copy in loads[2:]:
-        copy.wait()
-
-    @pl.loop(0, 2)
-    def _(m):
-        take_inputs(m)
+    take_inputs(1)
 
     for part in range(3):
         third[part].arrive(2, 3)
@@ -365,42 +366,49 @@
         before = old.astype(F32)
         fresh = (1.0 - update) * cand + update * before
         joined[at, 0:512] = fresh.astype(BF16)
-        delta = fresh - before
-        high = delta.astype(BF16)
-        dl[at, 0:512] = high
-        dl[at, 512:1024] = (delta - high.astype(F32)).astype(BF16)
+        dl[at, :] = (fresh - before).astype(BF16)
         xperm[at, :] = dot(inputs, perm[...]).astype(BF16)
 
-    for part in range(3):
+    results = [
+        pltpu.make_async_copy(dl, delta_ref, out_sem.at[0]),
+        pltpu.make_async_copy(locr, slots_ref, out_sem.at[1]),
+    ]
+    for copy in results:
+        copy.start()
+
+    def hidden_of(a, b):
+        up_y = lax.rem(y + a + a // 2 - 2 * (a // 3), RING)
+        up_x = lax.rem(x + b + b // 2 - 2 * (b // 3), RING)
+        at = pl.ds(pl.multiple_of(256 * (up_y * RING + up_x), 256), 256)
+        v = dot_nt(joined[...], win[up_y, up_x].reshape(256, 1024))
+        inner = v * (0.7978845608028654 + 0.035677408136300125 * (v * v))
+        hidden[:, at] = (v + v * jnp.tanh(inner)).astype(BF16)
+
+    for part in (1, 2):
+        for n in range(3):
+            lasts[part][n].wait_recv()
+
+    @pl.loop(0, 3)
+    def _(b):
+        hidden_of(0, b)
+
+    for part in (1, 2, 0):
         third[part].arrive(4, 5)
         lasts[part][3].start()
 
-    def update(m):
-        at = pl.ds(pl.multiple_of(512 * m, 512), 512)
-        owned = jnp.broadcast_to(locr[0:1, :], (512, 1024)).astype(jnp.int32)
-        mine = iota((512, 1024), 0) + (512 * m + 1) == owned
-        total2 = dot(one_hot(mine), dl[...])
-        count = jnp.sum(jnp.where(mine, 1.0, 0.0), axis=1, keepdims=True)
-        total = total2[:, 0:512] + total2[:, 512:1024]
-        st[at, :] = st[at, :] + total / jnp.maximum(count, 1.0)
-
-    @pl.loop(0, 2)
-    def _(m):
-        update(m)
-
-    for part in range(3):
-        for copy in lasts[part]:
-            copy.wait_recv()
-
-    @pl.loop(0, 16)
+    @pl.loop(3, 9)
     def _(j):
-        hid = pl.ds(pl.multiple_of(256 * j, 256), 256)
-        first = win[j // RING, lax.rem(j, RING)].reshape(256, 1024)
-        for m in range(2):
-            at = pl.ds(512 * m, 512)
-            v = dot_nt(joined[at, :], first)
-            inner = v * (0.7978845608028654 + 0.035677408136300125 * (v * v))
-            hidden[at, hid] = (v + v * jnp.tanh(inner)).astype(BF16)
+        hidden_of(j // 3, lax.rem(j, 3))
+
+    for part in (1, 2):
+        lasts[part][3].wait_recv()
+
+    @pl.loop(0, 7)
+    def _(j):
+        hidden_of(jnp.minimum(j, 3), jnp.where(j < 3, 3, j - 3))
+
+    for copy in lasts[0]:
+        copy.wait_recv()
 
     @pl.loop(0, 4)
     def _(m):
@@ -430,13 +438,9 @@
             copy.wait_send()
     settle(qsend, 16, 0)
     settle(qrecv, 8, 2)
-    update(2)
     settle(smid, 8, 5)
     spread(lambda p: smid.at[:, p], srecv, yx, 16, 6, to_plane)
     srecv[yx] = smid[:, yx]
-    update(3)
-    result = pltpu.make_async_copy(st, new_ref, out_sem)
-    result.start()
 
     settle(srecv, 16, 7)
     back = srecv[...].reshape(NDEV, 128)
@@ -452,7 +456,39 @@
     score_ref[...] = jnp.broadcast_to(score, (512, 128)).T[0:1, :]
     settle(ssend, 8, 4)
     settle(srecv, 16, 6)
-    result.wait()
+    for copy in results:
+        copy.wait()
+
+
+def update_kernel(states_ref, slots_ref, delta_ref, new_ref, st, slots, delta, in_sem, out_sem):
+    parts = 4
+    size = st.shape[0] // parts
+    blocks = [pl.ds(size * m, size) for m in range(parts)]
+    loads = [
+        pltpu.make_async_copy(slots_ref, slots, in_sem.at[parts]),
+        pltpu.make_async_copy(delta_ref, delta, in_sem.at[parts + 1]),
+    ]
+    arrivals = [
+        pltpu.make_async_copy(states_ref.at[at], st.at[at], in_sem.at[m]) for m, at in enumerate(blocks)
+    ]
+    results = [
+        pltpu.make_async_copy(st.at[at], new_ref.at[at], out_sem.at[m]) for m, at in enumerate(blocks)
+    ]
+    for copy in loads + arrivals:
+        copy.start()
+    loads[0].wait()
+    owned = jnp.broadcast_to(slots[0:1, :], (size, 1024)).astype(jnp.int32)
+    for m, at in enumerate(blocks):
+        mine = iota((size, 1024), 0) + (size * m + 1) == owned
+        count = jnp.sum(jnp.where(mine, 1.0, 0.0), axis=1, keepdims=True)
+        if m == 0:
+            loads[1].wait()
+        total = dot(one_hot(mine), delta[...])
+        arrivals[m].wait()
+        st[at, :] = st[at, :] + total / jnp.maximum(count, 1.0)
+        results[m].start()
+    for copy in results:
+        copy.wait()
 
 
 def per_device(
@@ -466,19 +502,19 @@
     tower_in,
     tower_out,
 ):
-    ids = jnp.stack([event_users, event_features])
     table = row_of_user.reshape(2048, 128)
     anywhere = pl.BlockSpec(memory_space=pl.ANY)
     vmem = pl.BlockSpec(memory_space=pltpu.VMEM)
     dma = pltpu.SemaphoreType.DMA
-    new_states, scores = pl.pallas_call(
+    delta, slots, scores = pl.pallas_call(
         kernel,
         out_shape=(
-            jax.ShapeDtypeStruct((2048, 512), F32),
+            jax.ShapeDtypeStruct((1024, 512), BF16),
+            jax.ShapeDtypeStruct((8, 1024), F32),
             jax.ShapeDtypeStruct((1, 512), F32),
         ),
-        in_specs=[vmem] + [anywhere] * 7,
-        out_specs=(anywhere, vmem),
+        in_specs=[vmem] * 2 + [anywhere] * 7,
+        out_specs=(anywhere, anywhere, vmem),
         scratch_shapes=[
             pltpu.VMEM((2048, 128), jnp.int32),
             pltpu.VMEM((2048, 512), F32),
@@ -503,13 +539,13 @@
             pltpu.VMEM((1024, 1024), BF16),
             pltpu.VMEM((1024, 512), BF16),
             pltpu.VMEM((1024, 512), BF16),
-            pltpu.VMEM((1024, 1024), BF16),
+            pltpu.VMEM((1024, 512), BF16),
             pltpu.VMEM((512, 512), BF16),
             pltpu.VMEM((1024, 4096), BF16),
             pltpu.VMEM((1024, 128), F32),
             dma((5,)),
             dma((3,)),
-            dma,
+            dma((2,)),
             dma((8,)),
             dma((3, 3)),
             dma((3, 3)),
@@ -523,7 +559,21 @@
         compiler_params=pltpu.CompilerParams(
             collective_id=0, has_side_effects=True, vmem_limit_bytes=60 * 1024 * 1024
         ),
-    )(ids, table, states, feature_table, gate_in, gate_state, tower_in, tower_out)
+    )(event_users.reshape(1, 512), event_features.reshape(1, 512), table, states, feature_table, gate_in, gate_state, tower_in, tower_out)
+    new_states = pl.pallas_call(
+        update_kernel,
+        out_shape=jax.ShapeDtypeStruct((2048, 512), F32),
+        in_specs=[anywhere] * 3,
+        out_specs=anywhere,
+        scratch_shapes=[
+            pltpu.VMEM((2048, 512), F32),
+            pltpu.VMEM((8, 1024), F32),
+            pltpu.VMEM((1024, 512), BF16),
+            dma((6,)),
+            dma((4,)),
+        ],
+        compiler_params=pltpu.CompilerParams(vmem_limit_bytes=60 * 1024 * 1024),
+    )(states, slots, delta)
     return new_states, scores.reshape(512)
 
 

time: 81.1 us -> 76.6 us (0.945)
  local copies, waits for them, and re-layouts: 5.22 us -> 0.58 us
  Pallas kernels: 73.7 us -> 75.2 us
  other arithmetic: 1.3 us -> 0 us
    unnamed x4 -> x3, local copies, waits for them, and re-layouts: 5.22 us -> 0.58 us
    pallas_call x1 -> x2, Pallas kernels: 73.7 us -> 75.2 us  [the longest x1 69.4 us: per_device(): pl.pallas_call(kernel, out_shape=(jax.ShapeDtypeStruct((1024, 512), BF16)...]
    another operation x1 -> x0, other arithmetic: 1.3 us -> none  [per_device(): ids = jnp.stack([event_users, event_features])]
where the time goes in v4:
time: 76.6 us; the launch traced here: 76.4 us
  Pallas kernels  75.2 us (98%)
    pallas_call x1, Pallas kernels, per_device(): pl.pallas_call(kernel, out_shape=(jax.ShapeDtypeStruct((1024, 512), BF16)...  69.4 us
    pallas_call x1, Pallas kernels, per_device(): pl.pallas_call(update_kernel, out_shape=jax.ShapeDtypeStruct((2048, 512),...  5.8 us

profile of v4, /device:TPU:1, one launch (start us, length us, event | category | flops | bytes accessed | tf_op | source)
XLA Modules:
  0.0 76.4 jit_solution(12298545426266603909)
XLA Ops:
  0.6 69.4 %shard_map.104 = (bf16[1024,512]{1,0:T(8,128)(2,1)}, f32[8,1024]{1,0:T(8,128)}, f32[1,512]{1,0:T(1,128)}) custom-call(s32[1,512]{1,0:T(1,128)} %bitcast.5, s32[1,512]{1,0:T(1,128)} %bitcast.6, s32[2048,128]{1,0:T(8,128)} %bitcast.4, f32[2048,512]{1,0:T(8,128)} %states_ref.3, bf16[4096,512]{1,0:T(8,128)(2,1)} %features_ref.1, bf16[512,1536]{1,0:T(8,128)(2,1)} %gate_in_ref.1, ...), custom_call_target="tpu_custom_call" | custom-call | tf_op jit(solution)/shard_map/pallas_call | solution.py:509
  70.0 0.0 copy-start
  70.0 5.8 %shard_map.105 = f32[2048,512]{1,0:T(8,128)} custom-call(f32[2048,512]{1,0:T(8,128)} %states_ref.3, f32[8,1024]{1,0:T(8,128)} %get-tuple-element.5.slots_ref, bf16[1024,512]{1,0:T(8,128)(2,1)} %get-tuple-element.6.delta_ref), custom_call_target="tpu_custom_call" | custom-call | tf_op jit(solution)/shard_map/pallas_call | solution.py:563
  75.8 0.0 copy-done
  75.9 0.6 copy.12
Async XLA Ops:
  70.0 5.8 %copy-start = (f32[1,512]{1,0:T(1,128)S(1)}, f32[1,512]{1,0:T(1,128)}, u32[]{:S(2)}) copy-start(f32[1,512]{1,0:T(1,128)} %get-tuple-element.7) | copy-start | bytes 6148

commit v5 on v4

--- a/solution.py
+++ b/solution.py
@@ -263,7 +263,7 @@
     requests = requests + 256.0 * pltpu.roll(requests, 128 - CAP, 1)
 
     def spread(src, dst, mine, count, n, to):
-        @pl.loop(1, count)
+        @pl.loop(1, count, unroll=True)
         def _(s):
             p = lax.rem(mine + s, count)
             remote(src(p), a2a_sem.at[n], a2a_sem.at[n + 1], to(p), dst.at[mine]).start()
@@ -280,7 +280,11 @@
         copy.wait()
     for copy in stage1:
         copy.wait_recv()
-    wout[y, z, c] = jnp.concatenate([raw[i].astype(F32) for i in range(RING)], axis=0).astype(BF16)
+    mine = jnp.concatenate([raw[i].astype(F32) for i in range(RING)], axis=0).astype(BF16)
+    j = iota((256, 256), 1)
+    order = one_hot(iota((256, 256), 0) == ((j & 127) >> 4) * 32 + (j >> 7) * 16 + (j & 15))
+    for g in range(16):
+        wout[y, z, c, :, 256 * g : 256 * (g + 1)] = dot(mine[:, 256 * g : 256 * (g + 1)], order).astype(BF16)
     for copy in stage2:
         copy.start()
 
@@ -376,43 +380,45 @@
     for copy in results:
         copy.start()
 
-    def hidden_of(a, b):
-        up_y = lax.rem(y + a + a // 2 - 2 * (a // 3), RING)
-        up_x = lax.rem(x + b + b // 2 - 2 * (b // 3), RING)
-        at = pl.ds(pl.multiple_of(256 * (up_y * RING + up_x), 256), 256)
-        v = dot_nt(joined[...], win[up_y, up_x].reshape(256, 1024))
-        inner = v * (0.7978845608028654 + 0.035677408136300125 * (v * v))
-        hidden[:, at] = (v + v * jnp.tanh(inner)).astype(BF16)
+    def activate(weights, store):
+        for m in range(2):
+            at = pl.ds(512 * m, 512)
+            v = dot_nt(joined[at, :], weights())
+            inner = v * (0.7978845608028654 + 0.035677408136300125 * (v * v))
+            done = (v + v * jnp.tanh(inner)).astype(BF16)
+            for i in range(RING):
+                hidden[at, pl.ds(pl.multiple_of(store(i), 128), 128)] = done[:, 128 * i : 128 * (i + 1)]
+
+    def unit(hop):
+        p = lax.rem(y + hop, RING)
+        q = lax.rem(x + hop, RING)
+        activate(lambda: win[p, :, :, :, 0].reshape(512, 1024), lambda i: 1024 * p + 256 * i)
+        activate(lambda: win[:, q, :, :, 1].reshape(512, 1024), lambda i: 1024 * i + 256 * q + 128)
 
     for part in (1, 2):
-        for n in range(3):
-            lasts[part][n].wait_recv()
-
-    @pl.loop(0, 3)
-    def _(b):
-        hidden_of(0, b)
+        lasts[part][0].wait_recv()
+    unit(0)
 
     for part in (1, 2, 0):
         third[part].arrive(4, 5)
         lasts[part][3].start()
-
-    @pl.loop(3, 9)
+    for part in (1, 2):
+        for n in (1, 2):
+            lasts[part][n].wait_recv()
+
+    @pl.loop(0, 2)
     def _(j):
-        hidden_of(j // 3, lax.rem(j, 3))
+        unit(1 + 2 * j)
 
     for part in (1, 2):
         lasts[part][3].wait_recv()
-
-    @pl.loop(0, 7)
-    def _(j):
-        hidden_of(jnp.minimum(j, 3), jnp.where(j < 3, 3, j - 3))
+    unit(2)
 
     for copy in lasts[0]:
         copy.wait_recv()
 
-    @pl.loop(0, 4)
-    def _(m):
-        at = pl.ds(pl.multiple_of(256 * m, 256), 256)
+    for m in range(2):
+        at = pl.ds(512 * m, 512)
         tower = dot_nt(hidden[at, :], wout[...].reshape(512, 4096))
         prod = tower * xperm[at, :].astype(F32)
         acc[at, :] = (prod[:, 0:128] + prod[:, 128:256]) + (prod[:, 256:384] + prod[:, 384:512])

time: 76.6 us -> 74.6 us (0.974)
  Pallas kernels: 75.2 us -> 73.2 us
    pallas_call x1, Pallas kernels: 69.4 us -> 67.4 us  [per_device(): pl.pallas_call(kernel, out_shape=(jax.ShapeDtypeStruct((1024, 512), BF16)...]
where the time goes in v5:
time: 74.6 us; the launch traced here: 74.5 us
  Pallas kernels  73.2 us (98%)
    pallas_call x1, Pallas kernels, per_device(): pl.pallas_call(kernel, out_shape=(jax.ShapeDtypeStruct((1024, 512), BF16)...  67.4 us
    pallas_call x1, Pallas kernels, per_device(): pl.pallas_call(update_kernel, out_shape=jax.ShapeDtypeStruct((2048, 512),...  5.8 us

profile of v5, /device:TPU:1, one launch (start us, length us, event | category | flops | bytes accessed | tf_op | source)
XLA Modules:
  0.0 74.5 jit_solution(4460165305587379498)
XLA Ops:
  0.6 67.4 %shard_map.104 = (bf16[1024,512]{1,0:T(8,128)(2,1)}, f32[8,1024]{1,0:T(8,128)}, f32[1,512]{1,0:T(1,128)}) custom-call(s32[1,512]{1,0:T(1,128)} %bitcast.5, s32[1,512]{1,0:T(1,128)} %bitcast.6, s32[2048,128]{1,0:T(8,128)} %bitcast.4, f32[2048,512]{1,0:T(8,128)} %states_ref.3, bf16[4096,512]{1,0:T(8,128)(2,1)} %features_ref.1, bf16[512,1536]{1,0:T(8,128)(2,1)} %gate_in_ref.1, ...), custom_call_target="tpu_custom_call" | custom-call | tf_op jit(solution)/shard_map/pallas_call | solution.py:515
  68.1 0.0 copy-start
  68.1 5.8 %shard_map.105 = f32[2048,512]{1,0:T(8,128)} custom-call(f32[2048,512]{1,0:T(8,128)} %states_ref.3, f32[8,1024]{1,0:T(8,128)} %get-tuple-element.5.slots_ref, bf16[1024,512]{1,0:T(8,128)(2,1)} %get-tuple-element.6.delta_ref), custom_call_target="tpu_custom_call" | custom-call | tf_op jit(solution)/shard_map/pallas_call | solution.py:569
  73.9 0.0 copy-done
  73.9 0.6 copy.12
Async XLA Ops:
  68.1 5.8 %copy-start = (f32[1,512]{1,0:T(1,128)S(1)}, f32[1,512]{1,0:T(1,128)}, u32[]{:S(2)}) copy-start(f32[1,512]{1,0:T(1,128)} %get-tuple-element.7) | copy-start | bytes 6148

commit v6 on v5

--- a/solution.py
+++ b/solution.py
@@ -42,8 +42,7 @@
     gate_state_ref,
     tin_ref,
     tout_ref,
-    delta_ref,
-    slots_ref,
+    mean_ref,
     score_ref,
     table,
     st,
@@ -71,6 +70,7 @@
     dl,
     perm,
     hidden,
+    means,
     acc,
     load_sem,
     own_sem,
@@ -373,12 +373,6 @@
         dl[at, :] = (fresh - before).astype(BF16)
         xperm[at, :] = dot(inputs, perm[...]).astype(BF16)
 
-    results = [
-        pltpu.make_async_copy(dl, delta_ref, out_sem.at[0]),
-        pltpu.make_async_copy(locr, slots_ref, out_sem.at[1]),
-    ]
-    for copy in results:
-        copy.start()
 
     def activate(weights, store):
         for m in range(2):
@@ -432,6 +426,20 @@
     ssend[...] = scores.reshape(8, 16, 1, 128)
     spread(lambda p: ssend.at[p], smid, zc, 8, 4, to_row)
     smid[zc] = ssend[zc]
+
+    owned = jnp.broadcast_to(locr[0:1, :], (512, 1024)).astype(jnp.int32)
+    results = []
+
+    def mean_of(m):
+        at = pl.ds(512 * m, 512)
+        matches = iota((512, 1024), 0) + (512 * m + 1) == owned
+        count = jnp.sum(jnp.where(matches, 1.0, 0.0), axis=1, keepdims=True)
+        means[at, :] = (dot(one_hot(matches), dl[...]) / jnp.maximum(count, 1.0)).astype(BF16)
+        results.append(pltpu.make_async_copy(means.at[at], mean_ref.at[at], out_sem.at[m]))
+        results[m].start()
+
+    mean_of(0)
+    mean_of(1)
 
     for copy in stage1:
         copy.wait_send()
@@ -447,6 +455,8 @@
     settle(smid, 8, 5)
     spread(lambda p: smid.at[:, p], srecv, yx, 16, 6, to_plane)
     srecv[yx] = smid[:, yx]
+    mean_of(2)
+    mean_of(3)
 
     settle(srecv, 16, 7)
     back = srecv[...].reshape(NDEV, 128)
@@ -466,34 +476,22 @@
         copy.wait()
 
 
-def update_kernel(states_ref, slots_ref, delta_ref, new_ref, st, slots, delta, in_sem, out_sem):
-    parts = 4
+def update_kernel(states_ref, mean_ref, new_ref, st, mean, in_sem, mean_sem, out_sem):
+    parts = 8
     size = st.shape[0] // parts
     blocks = [pl.ds(size * m, size) for m in range(parts)]
-    loads = [
-        pltpu.make_async_copy(slots_ref, slots, in_sem.at[parts]),
-        pltpu.make_async_copy(delta_ref, delta, in_sem.at[parts + 1]),
-    ]
-    arrivals = [
-        pltpu.make_async_copy(states_ref.at[at], st.at[at], in_sem.at[m]) for m, at in enumerate(blocks)
-    ]
-    results = [
-        pltpu.make_async_copy(st.at[at], new_ref.at[at], out_sem.at[m]) for m, at in enumerate(blocks)
-    ]
-    for copy in loads + arrivals:
-        copy.start()
-    loads[0].wait()
-    owned = jnp.broadcast_to(slots[0:1, :], (size, 1024)).astype(jnp.int32)
+    loads = [pltpu.make_async_copy(states_ref.at[at], st.at[at], in_sem.at[m]) for m, at in enumerate(blocks)]
+    adds = [pltpu.make_async_copy(mean_ref.at[at], mean.at[at], mean_sem.at[m]) for m, at in enumerate(blocks)]
+    stores = [pltpu.make_async_copy(st.at[at], new_ref.at[at], out_sem.at[m]) for m, at in enumerate(blocks)]
+    for m in range(parts):
+        loads[m].start()
+        adds[m].start()
     for m, at in enumerate(blocks):
-        mine = iota((size, 1024), 0) + (size * m + 1) == owned
-        count = jnp.sum(jnp.where(mine, 1.0, 0.0), axis=1, keepdims=True)
-        if m == 0:
-            loads[1].wait()
-        total = dot(one_hot(mine), delta[...])
-        arrivals[m].wait()
-        st[at, :] = st[at, :] + total / jnp.maximum(count, 1.0)
-        results[m].start()
-    for copy in results:
+        loads[m].wait()
+        adds[m].wait()
+        st[at, :] = st[at, :] + mean[at, :].astype(F32)
+        stores[m].start()
+    for copy in stores:
         copy.wait()
 
 
@@ -512,15 +510,14 @@
     anywhere = pl.BlockSpec(memory_space=pl.ANY)
     vmem = pl.BlockSpec(memory_space=pltpu.VMEM)
     dma = pltpu.SemaphoreType.DMA
-    delta, slots, scores = pl.pallas_call(
+    means, scores = pl.pallas_call(
         kernel,
         out_shape=(
-            jax.ShapeDtypeStruct((1024, 512), BF16),
-            jax.ShapeDtypeStruct((8, 1024), F32),
+            jax.ShapeDtypeStruct((2048, 512), BF16),
             jax.ShapeDtypeStruct((1, 512), F32),
         ),
         in_specs=[vmem] * 2 + [anywhere] * 7,
-        out_specs=(anywhere, anywhere, vmem),
+        out_specs=(anywhere, vmem),
         scratch_shapes=[
             pltpu.VMEM((2048, 128), jnp.int32),
             pltpu.VMEM((2048, 512), F32),
@@ -548,10 +545,11 @@
             pltpu.VMEM((1024, 512), BF16),
             pltpu.VMEM((512, 512), BF16),
             pltpu.VMEM((1024, 4096), BF16),
+            pltpu.VMEM((2048, 512), BF16),
             pltpu.VMEM((1024, 128), F32),
             dma((5,)),
             dma((3,)),
-            dma((2,)),
+            dma((4,)),
             dma((8,)),
             dma((3, 3)),
             dma((3, 3)),
@@ -569,17 +567,17 @@
     new_states = pl.pallas_call(
         update_kernel,
         out_shape=jax.ShapeDtypeStruct((2048, 512), F32),
-        in_specs=[anywhere] * 3,
+        in_specs=[anywhere] * 2,
         out_specs=anywhere,
         scratch_shapes=[
             pltpu.VMEM((2048, 512), F32),
-            pltpu.VMEM((8, 1024), F32),
-            pltpu.VMEM((1024, 512), BF16),
-            dma((6,)),
-            dma((4,)),
+            pltpu.VMEM((2048, 512), BF16),
+            dma((8,)),
+            dma((8,)),
+            dma((8,)),
         ],
         compiler_params=pltpu.CompilerParams(vmem_limit_bytes=60 * 1024 * 1024),
-    )(states, slots, delta)
+    )(states, means)
     return new_states, scores.reshape(512)
 
 

time: 74.6 us -> 73.6 us (0.987)
  Pallas kernels: 73.2 us -> 72.3 us
    pallas_call x1, Pallas kernels: 5.8 us -> 4.75 us  [per_device(): pl.pallas_call(update_kernel, out_shape=jax.ShapeDtypeStruct((2048, 512),...]
where the time goes in v6:
time: 73.6 us; the launch traced here: 73.5 us
  Pallas kernels  72.3 us (98%)
    pallas_call x1, Pallas kernels, per_device(): pl.pallas_call(kernel, out_shape=(jax.ShapeDtypeStruct((2048, 512), BF16)...  67.5 us
    pallas_call x1, Pallas kernels, per_device(): pl.pallas_call(update_kernel, out_shape=jax.ShapeDtypeStruct((2048, 512),...  4.75 us

profile of v6, /device:TPU:1, one launch (start us, length us, event | category | flops | bytes accessed | tf_op | source)
XLA Modules:
  0.0 73.5 jit_solution(17218775964128390240)
XLA Ops:
  0.6 67.5 %shard_map.104 = (bf16[2048,512]{1,0:T(8,128)(2,1)}, f32[1,512]{1,0:T(1,128)}) custom-call(s32[1,512]{1,0:T(1,128)} %bitcast.5, s32[1,512]{1,0:T(1,128)} %bitcast.6, s32[2048,128]{1,0:T(8,128)} %bitcast.4, f32[2048,512]{1,0:T(8,128)} %states_ref.3, bf16[4096,512]{1,0:T(8,128)(2,1)} %features_ref.1, bf16[512,1536]{1,0:T(8,128)(2,1)} %gate_in_ref.1, ...), custom_call_target="tpu_custom_call" | custom-call | tf_op jit(solution)/shard_map/pallas_call | solution.py:513
  68.2 0.0 copy-start
  68.2 4.7 %shard_map.105 = f32[2048,512]{1,0:T(8,128)} custom-call(f32[2048,512]{1,0:T(8,128)} %states_ref.3, bf16[2048,512]{1,0:T(8,128)(2,1)} %get-tuple-element.4.mean_ref), custom_call_target="tpu_custom_call" | custom-call | tf_op jit(solution)/shard_map/pallas_call | solution.py:567
  72.9 0.0 copy-done
  72.9 0.6 copy.12
Async XLA Ops:
  68.2 4.8 %copy-start = (f32[1,512]{1,0:T(1,128)S(1)}, f32[1,512]{1,0:T(1,128)}, u32[]{:S(2)}) copy-start(f32[1,512]{1,0:T(1,128)} %get-tuple-element.5) | copy-start | bytes 6148
